TPU v7x, 32 devices: a whole 2x2x4 slice. The times are simulated.
32 devices in a mesh: snp: 8 (over y, x, core), samp: 4 (over z).
Axes of the slice: x: 2, y: 2, z: 4, core: 2. Of those that a mesh axis runs over, the one named last changes fastest.
Arguments:
- genotypes: bfloat16 [2048, 2, 1024], P('samp', None, 'snp'), may hold values from 0.06 to 0.79, as said below
- case_labels: int32 [2048], P('samp'), may hold values from 0 to 1, as said below
- refit_own: int32 [128], P('snp'), may hold values from 0 to 127
- refit_peer: int32 [128], P('snp'), may hold values from 0 to 1023, as said below
Outputs:
- screen: float32 [1024, 4, 128], P(('snp', 'samp'))
- refit_stat: float32 [128], P('snp')
Inputs may be any that keep to these rules, and one draw needn't show every extreme that they name: `genotypes`: each entry is at least 0.06, and the two probabilities of a sample and SNP sum to at most 0.94. `case_labels`: both classes occur. `refit_peer`: within each aligned block of 16 entries (the pairs of one SNP block), at most 4 entries name SNPs of any one block of 128 SNPs, and some block is named exactly 4 times.
All inputs are finite; a program needn't handle non-finite values.
Results may differ from a plain program's by a relative error of at most 0.0035.
Values may be sent and summed in bfloat16 or wider, within the bound.
No kernel may reach another device: no remote copies, remote signals or barrier semaphores. Data moves between devices by JAX's collectives and lax.ppermute only.
A program may use at most 64 MiB of HBM per device.

v0:
```python
import jax
import jax.numpy as jnp
from jax import lax
from jax.sharding import PartitionSpec as P

HALF = 2
CAP = 4
ITERS = 10


def passed_along(value, axis, by):
    devices = lax.axis_size(axis)
    return lax.ppermute(value, axis, [(i, (i + by) % devices) for i in range(devices)])


def complete(inner_cells, margin_a, margin_b, totals):
    target = inner_cells.shape[:2] + inner_cells.shape[3:]
    margin_a = jnp.broadcast_to(margin_a, target)
    margin_b = jnp.broadcast_to(margin_b, target)
    third_col = margin_a - inner_cells[:, :, 0] - inner_cells[:, :, 1]
    third_row = margin_b - inner_cells[:, 0] - inner_cells[:, 1]
    corner = totals - margin_a[:, 0] - margin_a[:, 1] - third_row[:, 0] - third_row[:, 1]
    top_rows = jnp.concatenate([inner_cells, third_col[:, :, None]], axis=2)
    last_row = jnp.concatenate([third_row, corner[:, None]], axis=1)
    return jnp.concatenate([top_rows, last_row[:, None]], axis=1)


def kirkwood(table):
    pair_sum = jnp.sum(table, axis=0)
    class_a = jnp.sum(table, axis=2)
    class_b = jnp.sum(table, axis=1)
    single_a = jnp.sum(pair_sum, axis=1)
    single_b = jnp.sum(pair_sum, axis=0)
    class_sum = jnp.sum(class_a, axis=1)
    grand_total = jnp.sum(class_sum, axis=0)
    approx = (
        pair_sum[None]
        * class_a[:, :, None]
        * class_b[:, None, :]
        / (single_a[None, :, None] * single_b[None, None, :] * class_sum[:, None, None])
    )
    scale_sum = jnp.sum(approx, axis=(0, 1, 2))
    return 2.0 * jnp.sum(
        table * jnp.log(table * scale_sum / (grand_total * approx)), axis=(0, 1, 2)
    )


def refit(table):

    def sweep(number, fitted):
        fitted = fitted * (jnp.sum(table, axis=0) / jnp.sum(fitted, axis=0))[None]
        fitted = fitted * (jnp.sum(table, axis=2) / jnp.sum(fitted, axis=2))[:, :, None]
        fitted = fitted * (jnp.sum(table, axis=1) / jnp.sum(fitted, axis=1))[:, None]
        return fitted

    fitted = lax.fori_loop(0, ITERS, sweep, jnp.ones_like(table))
    return 2.0 * jnp.sum(table * jnp.log(table / fitted), axis=(0, 1, 2))


def tile_cells(owner, visitor, classes):
    samples = owner.shape[0]
    block = owner.shape[2]
    weighted = (visitor[:, None] * classes[:, :, None, None]).reshape(samples, 4 * block)
    product = lax.dot_general(
        owner.reshape(samples, 2 * block),
        weighted,
        (((0,), (0,)), ((), ())),
        preferred_element_type=jnp.float32,
    )
    return product.reshape(2, block, 2, 2, block)


def on_device(genotypes, case_labels, refit_own, refit_peer):
    samples = genotypes.shape[0]
    block = genotypes.shape[2]
    snp_count = lax.axis_size("snp")
    samp_count = lax.axis_size("samp")
    quarter = block // samp_count
    here = lax.axis_index("snp")
    slab_index = lax.axis_index("samp")
    weight = case_labels.astype(jnp.float32)
    classes = jnp.stack([weight, 1.0 - weight], axis=1).astype(jnp.bfloat16)
    margin_part = jnp.dot(
        classes.T, genotypes.reshape(samples, 2 * block), preferred_element_type=jnp.float32
    ).reshape(2, 2, block)
    count_part = jnp.sum(classes.astype(jnp.float32), axis=0)
    margin_own, counts = lax.psum((margin_part, count_part), "samp")
    margin = lax.all_gather(margin_own, "snp", axis=2, tiled=True)
    margin_rows = lax.dynamic_slice_in_dim(margin_own, slab_index * quarter, quarter, 2)[
        :, :, :, None
    ]
    totals = counts[:, None, None]
    behind = []
    visitor = genotypes
    for offset in range(1, HALF + 1):
        visitor = passed_along(visitor, "snp", 1)
        statistic_tile = tile_cells(genotypes, visitor, classes)
        margin_b = lax.dynamic_slice_in_dim(margin, (here - offset) % snp_count * block, block, 2)[
            :, :, None, :
        ]
        whole_tile = lax.psum(statistic_tile, "samp")
        row_cells = lax.dynamic_slice_in_dim(whole_tile, slab_index * quarter, quarter, 1)
        behind.append(
            kirkwood(complete(row_cells.transpose(2, 0, 3, 1, 4), margin_rows, margin_b, totals))
        )
    stacked = jnp.stack(behind).reshape(HALF, quarter, samp_count, quarter)
    swapped = lax.all_to_all(stacked, "samp", split_axis=2, concat_axis=1, tiled=True)
    flipped = swapped.reshape(HALF, block, quarter).transpose(0, 2, 1)
    ahead = []
    for offset in range(1, HALF + 1):
        ahead.append(passed_along(flipped[offset - 1], "snp", -offset))
    screen = jnp.stack(behind + ahead, axis=1)
    peer_block = refit_peer // block
    peer_local = refit_peer % block
    hits = (peer_block[:, None] == jnp.arange(snp_count)[None, :]).astype(jnp.int32)
    slot_rank = jnp.sum(hits * (jnp.cumsum(hits, axis=0) - 1), axis=1)
    slot_hit = (slot_rank[:, None] == jnp.arange(CAP)[None, :]).astype(jnp.int32)
    requests = jnp.sum(hits[:, :, None] * slot_hit[:, None, :] * peer_local[:, None, None], axis=0)
    requests = requests.reshape(snp_count * CAP)
    asked = lax.all_to_all(requests, "snp", split_axis=0, concat_axis=0, tiled=True)
    sent_cols = jnp.take(genotypes, asked, axis=2)
    got_cols = lax.all_to_all(sent_cols, "snp", split_axis=2, concat_axis=2, tiled=True)
    second_cols = jnp.take(got_cols, peer_block * CAP + slot_rank, axis=2).astype(jnp.float32)
    first_cols = jnp.take(genotypes, refit_own, axis=2).astype(jnp.float32)
    product = first_cols[:, :, None, :] * second_cols[:, None, :, :]
    cells_part = jnp.einsum(
        "sijr,sc->cijr", product, classes.astype(jnp.float32), precision=lax.Precision.HIGHEST
    )
    pair_cells = lax.psum(cells_part, "samp")
    own_global = here * block + refit_own
    table = complete(
        pair_cells, margin[:, :, own_global], margin[:, :, refit_peer], counts[:, None]
    )
    return (screen, refit(table))


def solution(mesh):
    in_specs = (P("samp", None, "snp"), P("samp"), P("snp"), P("snp"))
    out_specs = (P(("snp", "samp"), None, None), P("snp"))
    return jax.shard_map(
        on_device, mesh=mesh, in_specs=in_specs, out_specs=out_specs, check_vma=False
    )
```

profile of v0, /device:TPU:0, one launch (start us, length us, event | category | flops | bytes accessed | tf_op | source)
XLA Modules:
  0.0 144.1 jit_solution(10690287188710927559)
XLA Ops:
  7.7 0.7 compare_select_fusion.5
  8.9 0.7 copy.241
  9.6 5.1 %all-to-all-start.1 = ((s32[8,4,1]{1,2,0:T(1,128)}), s32[8,4,1]{1,2,0:T(1,128)S(1)}, u32[]{:S(2)}, u32[]{:S(2)}) async-start(s32[8,4,1]{1,2,0:T(1,128)} %copy.241), calls=%async_computation.1 | async-start | bytes 8192 | tf_op jit(solution)/shard_map/all_to_all | solution.py:120
  14.7 0.7 subtract_convert_fusion
  15.4 0.7 convert_convert_fusion
  16.1 1.3 copy.238
  17.8 1.0 copy.283
  19.2 0.6 gather_fusion
  20.1 0.7 gather_fusion.1
  21.3 0.7 reduce.37
  22.0 0.8 fusion.22
  22.8 4.2 %all-to-all-start.2 = ((bf16[512,2,32]{0,1,2:T(2,128)(2,1)}), bf16[512,2,32]{0,1,2:T(2,128)(2,1)S(1)}, u32[]{:S(2)}, u32[]{:S(2)}) async-start(bf16[512,2,32]{0,1,2:T(2,128)(2,1)} %fusion.22), calls=%async_computation.2 | async-start | bytes 131072 | tf_op jit(solution)/shard_map/all_to_all | solution.py:122
  27.1 5.0 %all-to-all-done.2 = bf16[512,2,32]{0,1,2:T(2,128)(2,1)S(1)} async-done(((bf16[512,2,32]{0,1,2:T(2,128)(2,1)}), bf16[512,2,32]{0,1,2:T(2,128)(2,1)S(1)}, u32[]{:S(2)}, u32[]{:S(2)}) %all-to-all-start.2) | async-done | bytes 65568 | tf_op jit(solution)/shard_map/all_to_all | solution.py:122
  32.0 0.6 gather_fusion.2
  33.1 12.1 %all-reduce = (f32[2,2,128]{2,0,1:T(2,128)S(1)}, f32[2]{0:T(128)S(1)}, f32[2,2,2,16]{3,0,2,1:T(2,128)S(1)}) all-reduce(f32[2,2,128]{2,0,1:T(2,128)S(1)} %fusion.36, f32[2]{0:T(128)S(1)} %get-tuple-element.132, f32[2,2,2,16]{3,0,2,1:T(2,128)S(1)} %fusion.14), channel_id=1, replica_groups=mesh['snp'=8,'samp'=4] {'samp'}, use_global_device_ids=true, to_apply=%region_1.0 | all-reduce | flops 642 | bytes 5136 | tf_op jit(solution)/shard_map/psum | solution.py:87
  45.2 8.0 %all_gather.3 = f32[2,2,1024]{2,0,1:T(2,128)S(1)} all-gather(f32[2,2,128]{2,0,1:T(2,128)S(1)} %get-tuple-element.107), channel_id=1, replica_groups=mesh['snp'=8,'samp'=4] {'snp'}, dimensions={2}, use_global_device_ids=true | all-gather | bytes 18432 | tf_op jit(solution)/shard_map/all_gather | solution.py:88
  53.8 0.6 gather_fusion.3
  55.7 6.2 %collective-permute-done.1 = bf16[512,2,128]{2,1,0:T(2,128)(2,1)S(1)} collective-permute-done((bf16[512,2,128]{2,1,0:T(2,128)(2,1)S(1)}, bf16[512,2,128]{2,1,0:T(2,128)(2,1)S(1)}, u32[]{:S(2)}, u32[]{:S(2)}) %collective-permute-start.1) | collective-permute-done | bytes 262176 | tf_op jit(solution)/shard_map/ppermute | solution.py:13
  61.9 3.3 %broadcast_multiply_fusion.1 = (bf16[512,2,2,128]{3,2,1,0:T(2,128)(2,1)S(1)}, bf16[512,2,2,128]{3,2,1,0:T(2,128)(2,1)S(1)}) fusion(bf16[512,2]{1,0:T(8,128)(2,1)S(1)} %copy.218, bf16[512,2,128]{2,1,0:T(2,128)(2,1)S(1)} %collective-permute-done, bf16[512,2,128]{2,1,0:T(2,128)(2,1)S(1)} %collective-permute-done.1), kind=kLoop, calls=%fused_computation.23 | loop fusion | flops 524288 | bytes 1574912 | tf_op jit(solution)/shard_map/mul | solution.py:63
  66.0 1.0 copy.227
  67.9 1.0 copy.219
  69.0 1.6 %while.13 = (s32[]{:T(128)}, f32[2,3,3,16]{3,0,2,1:T(2,128)S(1)}, f32[3,3,16]{2,1,0:T(4,128)S(1)}, f32[2,3,16]{2,0,1:T(2,128)S(1)}, f32[2,3,16]{2,0,1:T(2,128)S(1)}, /*index=5*/s32[]{:T(128)}, s32[]{:T(128)}) while((s32[]{:T(128)}, f32[2,3,3,16]{3,0,2,1:T(2,128)S(1)}, f32[3,3,16]{2,1,0:T(4,128)S(1)}, ...), condition=%wide.region_40.41_spmd.clone, body=%wide.region_36.40_spmd.clone.sunk | while | flops 3747 | bytes 14114 | solution.py:56
  70.8 47.4 %all-reduce.4.cloned.1.call-done = (f32[2,128,2,2,128]{4,1,3,2,0:T(8,128)}, f32[2,128,2,2,128]{4,1,3,0,2:T(8,128)}) async-done(((f32[2,128,2,2,128]{4,1,3,2,0:T(8,128)}, f32[2,128,2,2,128]{4,1,3,0,2:T(8,128)}), (f32[2,128,2,2,128]{4,1,3,2,0:T(8,128)}, f32[2,128,2,2,128]{4,1,3,0,2:T(8,128)})) %all-reduce.4.cloned.1.call-update) | async-done | bytes 1048592 | tf_op jit(solution)/shard_map/psum | solution.py:101
  118.2 0.9 fusion.53
  119.1 0.9 fusion.59
  121.3 0.7 reshape.381
  122.1 3.3 %all-to-all-start = ((f32[4,1,2048]{2,1,0:T(1,128)}), f32[4,1,2048]{2,1,0:T(1,128)S(1)}, u32[]{:S(2)}, u32[]{:S(2)}) async-start(f32[4,1,2048]{2,1,0:T(1,128)} %reshape.381), calls=%async_computation | async-start | bytes 65536 | tf_op jit(solution)/shard_map/all_to_all | solution.py:107
  125.4 5.6 %all-to-all-done = f32[4,1,2048]{2,1,0:T(1,128)S(1)} async-done(((f32[4,1,2048]{2,1,0:T(1,128)}), f32[4,1,2048]{2,1,0:T(1,128)S(1)}, u32[]{:S(2)}, u32[]{:S(2)}) %all-to-all-start) | async-done | bytes 32800 | tf_op jit(solution)/shard_map/all_to_all | solution.py:107
  131.5 0.7 reduce.38
  132.6 2.4 %collective-permute-start.3 = (f32[32,128]{1,0:T(8,128)S(1)}, f32[32,128]{1,0:T(8,128)S(1)}, u32[]{:S(2)}, u32[]{:S(2)}) collective-permute-start(f32[32,128]{1,0:T(8,128)S(1)} %get-tuple-element.148), channel_id=1, source_target_pairs={{0,24},{4,28},{8,0},{12,4},{16,8},{20,12},{24,16},{28,20},{1,25},{... | collective-permute-start | bytes 49160 | tf_op jit(solution)/shard_map/ppermute | solution.py:13
  135.6 0.8 collective-permute-done.3
  136.6 0.7 copy.254
  (171 shorter events, 10.7 us)
Async XLA Ops:
  7.2 48.0 %collective-permute-start = (bf16[512,2,128]{2,1,0:T(2,128)(2,1)}, bf16[512,2,128]{2,1,0:T(2,128)(2,1)S(1)}, u32[]{:S(2)}, u32[]{:S(2)}) collective-permute-start(bf16[512,2,128]{2,1,0:T(2,128)(2,1)} %param.6), channel_id=1, source_target_pairs={{0,4},{4,8},{8,12},{12,16},{16,20},{20,24},{24,28},{28,0},{1,5},{5... | collective-permute-start | bytes 786440 | tf_op jit(solution)/shard_map/ppermute | solution.py:13
  9.6 9.5 %copy-start.1 = (s32[16]{0:T(128)S(1)}, s32[16]{0:T(128)}, u32[]{:S(2)}) copy-start(s32[16]{0:T(128)} %param.8) | copy-start | bytes 196
  9.6 10.4 %all-to-all-start.1 = ((s32[8,4,1]{1,2,0:T(1,128)}), s32[8,4,1]{1,2,0:T(1,128)S(1)}, u32[]{:S(2)}, u32[]{:S(2)}) async-start(s32[8,4,1]{1,2,0:T(1,128)} %copy.241), calls=%async_computation.1 | async-start | bytes 8192 | tf_op jit(solution)/shard_map/all_to_all | solution.py:120
  22.8 9.2 %all-to-all-start.2 = ((bf16[512,2,32]{0,1,2:T(2,128)(2,1)}), bf16[512,2,32]{0,1,2:T(2,128)(2,1)S(1)}, u32[]{:S(2)}, u32[]{:S(2)}) async-start(bf16[512,2,32]{0,1,2:T(2,128)(2,1)} %fusion.22), calls=%async_computation.2 | async-start | bytes 131072 | tf_op jit(solution)/shard_map/all_to_all | solution.py:122
  27.0 91.2 %all-reduce.4.cloned.1.call-start = ((), (), s32[]{:S(2)}) async-start(), calls=%async_computation.3 | async-start | bytes 2097152 | tf_op jit(solution)/shard_map/psum | solution.py:101
  55.2 6.7 %collective-permute-start.1 = (bf16[512,2,128]{2,1,0:T(2,128)(2,1)S(1)}, bf16[512,2,128]{2,1,0:T(2,128)(2,1)S(1)}, u32[]{:S(2)}, u32[]{:S(2)}) collective-permute-start(bf16[512,2,128]{2,1,0:T(2,128)(2,1)S(1)} %collective-permute-done), channel_id=1, source_target_pairs={{0,4},{4,8},{8,12},{12,16},{16,20},{20,24},{24,28},{28,0},{1,5},{5... | collective-permute-start | bytes 786440 | tf_op jit(solution)/shard_map/ppermute | solution.py:13
  55.7 9.7 %copy-start = (bf16[512,2,128]{2,1,0:T(2,128)(2,1)S(1)}, bf16[512,2,128]{2,1,0:T(2,128)(2,1)}, u32[]{:S(2)}) copy-start(bf16[512,2,128]{2,1,0:T(2,128)(2,1)} %param.6) | copy-start | bytes 786436
  122.1 8.9 %all-to-all-start = ((f32[4,1,2048]{2,1,0:T(1,128)}), f32[4,1,2048]{2,1,0:T(1,128)S(1)}, u32[]{:S(2)}, u32[]{:S(2)}) async-start(f32[4,1,2048]{2,1,0:T(1,128)} %reshape.381), calls=%async_computation | async-start | bytes 65536 | tf_op jit(solution)/shard_map/all_to_all | solution.py:107
  132.6 3.9 %collective-permute-start.3 = (f32[32,128]{1,0:T(8,128)S(1)}, f32[32,128]{1,0:T(8,128)S(1)}, u32[]{:S(2)}, u32[]{:S(2)}) collective-permute-start(f32[32,128]{1,0:T(8,128)S(1)} %get-tuple-element.148), channel_id=1, source_target_pairs={{0,24},{4,28},{8,0},{12,4},{16,8},{20,12},{24,16},{28,20},{1,25},{... | collective-permute-start | bytes 49160 | tf_op jit(solution)/shard_map/ppermute | solution.py:13
  135.0 1.6 %collective-permute-start.2 = (f32[32,128]{1,0:T(8,128)S(1)}, f32[32,128]{1,0:T(8,128)S(1)}, u32[]{:S(2)}, u32[]{:S(2)}) collective-permute-start(f32[32,128]{1,0:T(8,128)S(1)} %get-tuple-element.147), channel_id=1, source_target_pairs={{0,28},{4,0},{8,4},{12,8},{16,12},{20,16},{24,20},{28,24},{1,29},{... | collective-permute-start | bytes 49160 | tf_op jit(solution)/shard_map/ppermute | solution.py:13
Sparse Core Ops, SparseCore 0:
  69.1 49.0 all-reduce.3
where the time goes:
time: 145 us; the launch traced here: 144 us
  waiting for transfers between devices  65.2 us (45%)
  blocking collectives  20.1 us (14%)
  starting transfers between devices  16 us (11%)
  between operations  14.6 us (10%)
  local copies, waits for them, and re-layouts  13.8 us (10%)
  other arithmetic  12.9 us (9%)
    psum x1, waiting for transfers between devices, on_device(): whole_tile = lax.psum(statistic_tile, 'samp')  47.4 us
    psum x1, blocking collectives, on_device(): margin_own, counts = lax.psum((margin_part, count_part), 'samp')  12.1 us
    all_gather x1, blocking collectives, on_device(): margin = lax.all_gather(margin_own, 'snp', axis=2, tiled=True)  8.02 us
    ppermute x4, waiting for transfers between devices, passed_along(): lax.ppermute(value, axis, [(i, (i + by) % devices) for i in range(devices)])  7.15 us
    all_to_all x1, waiting for transfers between devices, on_device(): lax.all_to_all(stacked, 'samp', split_axis=2, concat_axis=1, tiled=True)  5.58 us
    all_to_all x1, starting transfers between devices, on_device(): lax.all_to_all(requests, 'snp', split_axis=0, concat_axis=0, tiled=True)  5.12 us
    all_to_all x1, waiting for transfers between devices, on_device(): lax.all_to_all(sent_cols, 'snp', split_axis=2, concat_axis=2, tiled=True)  4.96 us
    all_to_all x1, starting transfers between devices, on_device(): lax.all_to_all(sent_cols, 'snp', split_axis=2, concat_axis=2, tiled=True)  4.2 us
  transfers between devices with their start and end apart: 8, of which 6 were waited for; matrix products, arithmetic and copies ran while one was open for 10% of the time, Pallas kernels for 0%

commit v1 on v0

v1 whole, which is shorter than its diff:
```python
import functools

import jax
import jax.numpy as jnp
from jax import lax
from jax.experimental import pallas as pl
from jax.experimental.pallas import tpu as pltpu
from jax.sharding import PartitionSpec as P

HALF = 2
CAP = 4
ITERS = 10
MIDDLE = 0.47
SPREAD = 0.411
F32 = jnp.float32
BF16 = jnp.bfloat16


def iota(shape, axis):
    return lax.broadcasted_iota(jnp.int32, shape, axis)


def by_t(a, b):
    return lax.dot_general(a, b, (((1,), (1,)), ((), ())), preferred_element_type=F32)


def dot(a, b):
    return lax.dot_general(a, b, (((1,), (0,)), ((), ())), preferred_element_type=F32)


def earlier(count):
    return (iota((count, count), 0) < iota((count, count), 1)).astype(BF16)


def split_genotypes(ref, wide):
    rows = wide.shape[0]
    wide[...] = ref[0:rows, :].astype(F32)
    return [wide[pl.ds(j, rows // 2, stride=2), :] for j in range(2)]


def select_kernel(ids, geno, sent, wide, *, shift):
    here = lax.axis_index("snp")
    blocks, pairs = ids.shape
    block = geno.shape[1]
    rows = blocks * 2 * CAP
    names = ids[...]
    local = (names & (block - 1)).astype(F32)
    hit = (lax.shift_right_logical(names, shift) == here).astype(F32)
    rank = dot(hit.astype(BF16), earlier(pairs))
    spread = (lax.shift_right_logical(iota((rows, blocks), 0), 3) == iota((rows, blocks), 1)).astype(BF16)
    hit_rows = dot(spread, hit.astype(BF16))
    rank_rows = dot(spread, rank.astype(BF16))
    local_rows = dot(spread, local.astype(BF16))
    slot = (iota((rows, pairs), 0) & (CAP - 1)).astype(F32)
    chosen = jnp.where(rank_rows == slot, hit_rows, 0.0)
    column = jnp.sum(chosen * local_rows, axis=1, keepdims=True)
    valid = jnp.sum(chosen, axis=1, keepdims=True)
    which = iota((rows, block), 1).astype(F32)
    second = (iota((rows, block), 0) & CAP) > 0
    one_hot = jnp.where((which == column) & (valid > 0.5), 1.0, 0.0)
    low = jnp.where(second, 0.0, one_hot).astype(BF16)
    high = jnp.where(second, one_hot, 0.0).astype(BF16)
    g0, g1 = split_genotypes(geno, wide)
    sent[...] = (by_t(low, g0.astype(BF16)) + by_t(high, g1.astype(BF16))).astype(BF16)


def fixed(value, samples):
    return (value * 2.0 ** (30 - (samples - 1).bit_length())).astype(jnp.int32)


def floating(value, samples):
    return value.astype(F32) * 2.0 ** ((samples - 1).bit_length() - 30)


def code_step(count):
    return jnp.maximum(count, 1.0) * (SPREAD * SPREAD / 32767.0)


def quantized(value, step):
    scaled = value * (1.0 / step)
    return jnp.clip(jnp.floor(scaled + 0.5), -32767.0, 32767.0).astype(jnp.int32)


def class_rows(label0, tail):
    case0 = label0[...].astype(F32)
    case1 = jnp.concatenate([tail[q:q + 1, :].astype(F32) for q in range(case0.shape[1] // tail.shape[1])], axis=1)
    case = jnp.concatenate([case0, case1], axis=1)
    return [case, 1.0 - case]


def coded_tiles(first_refs, second_refs, classes, left, right, wide, outs):
    k = lax.axis_index("samp")
    samples = wide.shape[0] // 2
    block = wide.shape[1]
    quarter = block // 4
    first_slab = None
    for half in range(2):
        rows = pl.ds(half * samples, samples)
        parts = split_genotypes(first_refs[half], wide)
        if half == 0:
            first_slab = [p.astype(BF16) for p in parts]
        for i in range(2):
            turned = parts[i].T
            for c in range(2):
                piece = (turned * classes[c][:, half * samples:(half + 1) * samples]).astype(BF16)
                for q in range(4):
                    d = (q + 4 - k) & 3
                    left[d, c * 2 + i, :, rows] = piece[q * quarter:(q + 1) * quarter]
        parts = split_genotypes(second_refs[half], wide)
        for j in range(2):
            right[rows, j * block:(j + 1) * block] = parts[j].astype(BF16)
    lhs = left[...].reshape(16 * quarter, 2 * samples)
    cells = dot(lhs, right[...])
    row_sums = dot(lhs, jnp.ones((2 * samples, block), BF16))
    weights = jnp.concatenate(classes + [jnp.zeros((6, 2 * samples), F32)], axis=0).astype(BF16)
    column_sums = dot(weights, right[...])
    lanes = jnp.ones((1, 2 * block), F32)
    counts = [jnp.sum(classes[c], axis=1, keepdims=True) * lanes for c in range(2)]
    for d in range(4):
        words = None
        for c in range(2):
            rows = slice((d * 2 + c) * 2 * quarter, (d * 2 + c + 1) * 2 * quarter)
            row = row_sums[rows]
            base = jnp.concatenate([row, row], axis=1)
            centred = cells[rows] - MIDDLE * (base + column_sums[c:c + 1]) + (MIDDLE * MIDDLE) * counts[c]
            code = quantized(centred, code_step(counts[c]))
            words = lax.shift_left(code, 16) if c == 0 else words | (code & 0xFFFF)
        outs[d][0:2 * quarter, :] = words
    return first_slab, column_sums, counts


def write_tails(outs, start, samples, columns, own, counts):
    parts = [fixed(v, 2 * samples) for v in (columns[0:2], own[0:2], counts[0], counts[1])]
    tail = jnp.concatenate(parts + [jnp.zeros((2, columns.shape[1]), jnp.int32)], axis=0)
    for out in outs:
        out[start:start + 8, :] = tail


def ahead_kernel(own0, own1, other0, other1, label0, a0, a1, a2, a3, sums, wide, left, right):
    samples = wide.shape[0] // 2
    classes = class_rows(label0, own1[2 * samples:, :])
    outs = (a0, a1, a2, a3)
    _, columns, counts = coded_tiles((other0, other1), (own0, own1), classes, left, right, wide, outs)
    write_tails(outs, wide.shape[1] // 2, samples, columns, columns, counts)
    sums[...] = columns


def behind_kernel(own0, own1, other0, other1, label0, own_ids, peer_ids, got, sums,
                  b0, b1, b2, b3, wide, left, right, *, shift):
    samples = wide.shape[0] // 2
    block = wide.shape[1]
    classes = class_rows(label0, own1[2 * samples:, :])
    outs = (b0, b1, b2, b3)
    own_slab, columns, counts = coded_tiles((own0, own1), (other0, other1), classes, left, right, wide, outs)
    write_tails(outs, block // 2, samples, columns, sums[...], counts)

    pairs = peer_ids.shape[1]
    rows = got.shape[0]
    blocks = rows // (2 * CAP)
    peers = lax.shift_right_logical(peer_ids[...], shift)
    member = (iota((blocks, pairs), 0) == peers).astype(F32)
    before = dot(member.astype(BF16), earlier(pairs))
    rank = jnp.sum(member * before, axis=0, keepdims=True)
    row = iota((rows, pairs), 0)
    row_block = lax.shift_right_logical(row, 3)
    row_slot = (row & (2 * CAP - 1)).astype(F32)
    first_pick = (iota((block, pairs), 0) == own_ids[...]).astype(F32).T.astype(BF16)
    first, second = [], []
    for j in range(2):
        pick = jnp.where((row_block == peers) & (row_slot == rank + float(CAP * j)), 1.0, 0.0).T.astype(BF16)
        second.append(dot(pick, got[...]))
        first.append(by_t(first_pick, own_slab[j]))
    slab = [classes[c][:, 0:samples] for c in range(2)]
    values = []
    for c in range(2):
        for i in range(2):
            mine = first[i] * slab[c]
            for j in range(2):
                values.append(jnp.sum(mine * second[j], axis=1, keepdims=True))
    for side in (first, second):
        for c in range(2):
            for i in range(2):
                values.append(jnp.sum(side[i] * slab[c], axis=1, keepdims=True))
    lane = iota((pairs, 2 * block), 1)
    refit = jnp.zeros((pairs, 2 * block), F32)
    for v, value in enumerate(values):
        refit = jnp.where(lane == v, value, refit)
    refit = fixed(refit, 2 * samples)
    for out in outs:
        out[block // 2 + 8:, :] = refit


def complete(cells, margin_a, margin_b, totals):
    table = [[[None] * 3 for _ in range(3)] for _ in range(2)]
    for c in range(2):
        n = table[c]
        for i in range(2):
            for j in range(2):
                n[i][j] = cells[c][i][j]
            n[i][2] = margin_a[c][i] - n[i][0] - n[i][1]
        for j in range(2):
            n[2][j] = margin_b[c][j] - n[0][j] - n[1][j]
        n[2][2] = (totals[c] - margin_a[c][0] - margin_a[c][1]) - n[2][0] - n[2][1]
    return table


def kirkwood(n, margin_a, margin_b, totals):
    row_ic = [[margin_a[c][0], margin_a[c][1], totals[c] - margin_a[c][0] - margin_a[c][1]] for c in range(2)]
    col_jc = [[margin_b[c][0], margin_b[c][1], totals[c] - margin_b[c][0] - margin_b[c][1]] for c in range(2)]
    single_a = [row_ic[0][i] + row_ic[1][i] for i in range(3)]
    single_b = [col_jc[0][j] + col_jc[1][j] for j in range(3)]
    grand = totals[0] + totals[1]
    inv_a = [1.0 / s for s in single_a]
    row_x = [[row_ic[c][i] * inv_a[i] / totals[c] for i in range(3)] for c in range(2)]
    col_y = [[col_jc[c][j] / single_b[j] for j in range(3)] for c in range(2)]
    scale = None
    approx = {}
    for i in range(3):
        for j in range(3):
            pair = n[0][i][j] + n[1][i][j]
            for c in range(2):
                value = pair * row_x[c][i] * col_y[c][j]
                approx[c, i, j] = value
                scale = value if scale is None else scale + value
    factor = scale / grand
    total = None
    for (c, i, j), value in approx.items():
        term = n[c][i][j] * jnp.log(n[c][i][j] * factor / value)
        total = term if total is None else total + term
    return 2.0 * total


def finish_kernel(b0, b1, b2, b3, a0, a1, a2, a3, screen, stat, columns, *, samples):
    k = lax.axis_index("samp")
    bs, as_ = (b0, b1, b2, b3), (a0, a1, a2, a3)
    block = b0.shape[1] // 2
    quarter = block // 4
    height = 2 * quarter
    pairs = stat.shape[1]

    def both(x, y, row, lanes=slice(0, block)):
        return floating(x[row:row + 1, lanes], 2 * samples) + floating(y[row:row + 1, lanes], 2 * samples)

    lanes_of = [slice(j * block, (j + 1) * block) for j in range(2)]
    totals_row = [both(b0, b2, height + 4 + c) for c in range(2)]
    own = [both(b0, b2, height + 2 + c, lanes_of[i]) for c in range(2) for i in range(2)]
    columns[...] = jnp.concatenate(own + [jnp.zeros((block - 4, block), F32)], axis=0).T
    mine = columns[pl.ds(pl.multiple_of(k * quarter, quarter), quarter), :]
    margin_a = [[jnp.broadcast_to(mine[:, c * 2 + i:c * 2 + i + 1], (quarter, block)) for i in range(2)] for c in range(2)]

    stats = []
    for msgs in (bs, as_):
        for parity in range(2):
            x, y = msgs[parity], msgs[parity + 2]
            steps = [[code_step(floating(m[height + 4 + c:height + 5 + c, 0:block], 2 * samples)) for m in (x, y)]
                     for c in range(2)]
            margin_b = [[both(x, y, height + c, lanes_of[j]) for j in range(2)] for c in range(2)]
            cells = [[[None, None], [None, None]] for _ in range(2)]
            for i in range(2):
                for j in range(2):
                    words = [m[i * quarter:(i + 1) * quarter, lanes_of[j]] for m in (x, y)]
                    for c in range(2):
                        codes = [lax.shift_right_arithmetic(w if c == 0 else lax.shift_left(w, 16), 16) for w in words]
                        base = MIDDLE * (margin_a[c][i] + margin_b[c][j]) - (MIDDLE * MIDDLE) * totals_row[c]
                        cells[c][i][j] = (codes[0].astype(F32) * steps[c][0] + codes[1].astype(F32) * steps[c][1]) + base
            table = complete(cells, margin_a, margin_b, totals_row)
            stats.append(kirkwood(table, margin_a, margin_b, totals_row))
    even = (k & 1) == 0
    for side in range(2):
        e, o = stats[2 * side], stats[2 * side + 1]
        screen[:, 2 * side, :] = jnp.where(even, e, o)
        screen[:, 2 * side + 1, :] = jnp.where(even, o, e)

    for start in range(0, pairs, block):
        count = min(block, pairs - start)
        rows = slice(height + 8 + start, height + 8 + start + count)
        sums = sum(floating(m[rows, 0:block], 2 * samples) for m in bs[1:]) + floating(b0[rows, 0:block], 2 * samples)
        if count < block:
            sums = jnp.concatenate([sums, jnp.ones((block - count, block), F32)], axis=0)
        turned = sums.T
        row = [turned[v:v + 1, :] for v in range(16)]
        cells = [[[row[c * 4 + i * 2 + j] for j in range(2)] for i in range(2)] for c in range(2)]
        ma = [[row[8 + c * 2 + i] for i in range(2)] for c in range(2)]
        mb = [[row[12 + c * 2 + j] for j in range(2)] for c in range(2)]
        n = complete(cells, ma, mb, totals_row)
        n_ij = [[n[0][i][j] + n[1][i][j] for j in range(3)] for i in range(3)]
        n_ic = [[n[c][i][0] + n[c][i][1] + n[c][i][2] for i in range(3)] for c in range(2)]
        n_jc = [[n[c][0][j] + n[c][1][j] + n[c][2][j] for j in range(3)] for c in range(2)]

        def sweep(_, flat):
            f = [[[flat[c * 9 + i * 3 + j] for j in range(3)] for i in range(3)] for c in range(2)]
            for i in range(3):
                for j in range(3):
                    ratio = n_ij[i][j] / (f[0][i][j] + f[1][i][j])
                    for c in range(2):
                        f[c][i][j] = f[c][i][j] * ratio
            for c in range(2):
                for i in range(3):
                    ratio = n_ic[c][i] / (f[c][i][0] + f[c][i][1] + f[c][i][2])
                    for j in range(3):
                        f[c][i][j] = f[c][i][j] * ratio
                for j in range(3):
                    ratio = n_jc[c][j] / (f[c][0][j] + f[c][1][j] + f[c][2][j])
                    for i in range(3):
                        f[c][i][j] = f[c][i][j] * ratio
            return tuple(f[c][i][j] for c in range(2) for i in range(3) for j in range(3))

        fitted = lax.fori_loop(0, ITERS, sweep, tuple(jnp.ones((1, block), F32) for _ in range(18)))
        total = None
        for c in range(2):
            for i in range(3):
                for j in range(3):
                    term = n[c][i][j] * jnp.log(n[c][i][j] / fitted[c * 9 + i * 3 + j])
                    total = term if total is None else total + term
        stat[:, start:start + count] = (2.0 * total)[:, 0:count]


def vmem(count):
    return [pl.BlockSpec(memory_space=pltpu.VMEM)] * count


def run(body, args, outs, scratch):
    return pl.pallas_call(
        body,
        out_shape=outs,
        in_specs=vmem(len(args)),
        out_specs=jax.tree.map(lambda _: pl.BlockSpec(memory_space=pltpu.VMEM), outs),
        scratch_shapes=scratch,
    )(*args)


def on_device(genotypes, case_labels, refit_own, refit_peer):
    samples, _, block = genotypes.shape
    pairs = refit_peer.shape[0]
    snp_count = lax.axis_size("snp")
    samp_count = lax.axis_size("samp")
    assert samp_count == 2 * HALF and block & (block - 1) == 0
    shift = block.bit_length() - 1
    here = lax.axis_index("snp")

    def moved(value, where):
        links = []
        for b in range(snp_count):
            for k in range(samp_count):
                to_b, to_k = where(b, k)
                links.append((b * samp_count + k, (to_b % snp_count) * samp_count + to_k % samp_count))
        return lax.ppermute(value, ("snp", "samp"), links)

    geno = genotypes.reshape(2 * samples, block)
    labels = case_labels.reshape(1, samples)
    marks = jnp.pad(case_labels.astype(BF16).reshape(samples // block, block), ((0, -(samples // block) % 8), (0, 0)))
    other0 = moved(geno, lambda b, k: (b + 1 + (k & 1), k))
    other1 = moved(geno, lambda b, k: (b + 2 - (k & 1), k ^ 1))
    own1 = moved(jnp.concatenate([geno, marks], axis=0), lambda b, k: (b, k ^ 1))
    ids = lax.psum(jnp.where(iota((snp_count, pairs), 0) == here, refit_peer[None, :], 0), "snp")
    wide = pltpu.VMEM((2 * samples, block), F32)
    sent = run(
        functools.partial(select_kernel, shift=shift), (ids, geno),
        jax.ShapeDtypeStruct((snp_count * 2 * CAP, samples), BF16), [wide],
    )
    got = lax.all_to_all(sent, "snp", split_axis=0, concat_axis=0, tiled=True)
    scratch = [wide, pltpu.VMEM((4, 4, block // 4, 2 * samples), BF16), pltpu.VMEM((2 * samples, 2 * block), BF16)]
    short = jax.ShapeDtypeStruct((block // 2 + 8, 2 * block), jnp.int32)
    tall = jax.ShapeDtypeStruct((block // 2 + 8 + pairs, 2 * block), jnp.int32)
    *ahead, sums = run(
        ahead_kernel, (geno, own1, other0, other1, labels),
        [short] * 4 + [jax.ShapeDtypeStruct((8, 2 * block), F32)], scratch,
    )
    for d in range(4):
        ahead[d] = moved(ahead[d], lambda b, k: (b - 1 - (k & 1), k + d))
    behind = run(
        functools.partial(behind_kernel, shift=shift),
        (geno, own1, other0, other1, labels, refit_own[None, :], refit_peer[None, :], got, sums),
        [tall] * 4, scratch,
    )
    behind = list(behind)
    for d in range(1, 4):
        behind[d] = moved(behind[d], lambda b, k: (b, k + d))
    screen, stat = run(
        functools.partial(finish_kernel, samples=samples), (*behind, *ahead),
        [jax.ShapeDtypeStruct((block // samp_count, 2 * HALF, block), F32), jax.ShapeDtypeStruct((1, pairs), F32)],
        [pltpu.VMEM((block, block), F32)],
    )
    return screen, stat.reshape(pairs)


def solution(mesh):
    in_specs = (P("samp", None, "snp"), P("samp"), P("snp"), P("snp"))
    out_specs = (P(("snp", "samp"), None, None), P("snp"))
    return jax.shard_map(on_device, mesh=mesh, in_specs=in_specs, out_specs=out_specs, check_vma=False)
```

time: 145 us -> 57.1 us (0.39)
  waiting for transfers between devices: 65.2 us -> 7.06 us
  between operations: 14.6 us -> 0.8 us
  blocking collectives: 20.1 us -> 8.1 us
  Pallas kernels: 0 us -> 12 us
  other arithmetic: 12.9 us -> 1.73 us
  local copies, waits for them, and re-layouts: 13.8 us -> 2.82 us
  starting transfers between devices: 16 us -> 24.1 us
    psum x1 -> x0, waiting for transfers between devices: 47.4 us -> none  [on_device(): whole_tile = lax.psum(statistic_tile, 'samp')]
    ppermute x4 -> x10, starting transfers between devices: 3.37 us -> 20.8 us  [moved(): return lax.ppermute(value, ('snp', 'samp'), links)]
    pallas_call x0 -> x4, Pallas kernels: none -> 12 us  [run(): pl.pallas_call(body, out_shape=outs, in_specs=vmem(len(args)), out_specs=...]
    all_to_all x3 -> x1, waiting for transfers between devices: 10.5 us -> 0.01 us  [on_device(): got = lax.all_to_all(sent, 'snp', split_axis=0, concat_axis=0, tiled=True)]
    all_to_all x3 -> x1, starting transfers between devices: 12.6 us -> 3.35 us  [on_device(): got = lax.all_to_all(sent, 'snp', split_axis=0, concat_axis=0, tiled=True)]
    all_gather x1 -> x0, blocking collectives: 8.02 us -> none  [on_device(): margin = lax.all_gather(margin_own, 'snp', axis=2, tiled=True)]
    reduce_sum x55 -> x0, other arithmetic: 4.01 us -> none  [the longest x5 1.97 us: kirkwood(): class_sum = jnp.sum(class_a, axis=1)]
    mul x16 -> x0, other arithmetic: 4.01 us -> none  [the longest x1 3.26 us: tile_cells(): visitor[:, None] * classes[:, :, None, None]]
  transfers between devices with their start and end apart: 8 -> 11, of which waited for: 6 -> 1; matrix products, arithmetic and copies ran while one was open for 10% -> 3% of each run, Pallas kernels for 0% -> 16%
where the time goes in v1:
time: 57.1 us; the launch traced here: 56.7 us
  starting transfers between devices  24.1 us (42%)
  Pallas kernels  12 us (21%)
  blocking collectives  8.1 us (14%)
  waiting for transfers between devices  7.06 us (12%)
  local copies, waits for them, and re-layouts  2.82 us (5%)
  other arithmetic  1.73 us (3%)
  between operations  0.8 us (1%)
    ppermute x10, starting transfers between devices, moved(): return lax.ppermute(value, ('snp', 'samp'), links)  20.8 us
    pallas_call x4, Pallas kernels, run(): pl.pallas_call(body, out_shape=outs, in_specs=vmem(len(args)), out_specs=...  12 us
    psum x1, blocking collectives, on_device(): lax.psum(jnp.where(iota((snp_count, pairs), 0) == here, refit_peer[None,...  8.1 us
    ppermute x10, waiting for transfers between devices, moved(): return lax.ppermute(value, ('snp', 'samp'), links)  7.06 us
    all_to_all x1, starting transfers between devices, on_device(): got = lax.all_to_all(sent, 'snp', split_axis=0, concat_axis=0, tiled=True)  3.35 us
    unnamed x28, local copies, waits for them, and re-layouts  2.82 us
  transfers between devices with their start and end apart: 11, of which 1 were waited for; matrix products, arithmetic and copies ran while one was open for 3% of the time, Pallas kernels for 16%

profile of v1, /device:TPU:0, one launch (start us, length us, event | category | flops | bytes accessed | tf_op | source)
XLA Modules:
  0.0 56.7 jit_solution(5547194049151734686)
XLA Ops:
  0.6 4.0 %collective-permute-start.2 = (bf16[1024,128]{1,0:T(8,128)(2,1)}, bf16[1024,128]{1,0:T(8,128)(2,1)S(1)}, u32[]{:S(2)}, u32[]{:S(2)}) collective-permute-start(bf16[1024,128]{1,0:T(8,128)(2,1)} %bitcast.9), channel_id=1, source_target_pairs={{0,9},{1,4},{2,11},{3,6},{4,13},{5,8},{6,15},{7,10},{8,17},{9,12},... | collective-permute-start | bytes 786440 | tf_op jit(solution)/shard_map/ppermute | solution.py:347
  4.7 0.0 collective-permute-start.1
  4.7 0.7 %convert_bitcast_fusion = bf16[4,128]{1,0:T(4,128)(2,1)S(1)} fusion(s32[512]{0:T(512)} %param.5), kind=kLoop, calls=%fused_computation.4 | loop fusion | flops 512 | bytes 3072 | tf_op jit(solution)/shard_map/reshape | solution.py:351
  5.4 1.0 %fusion.1 = bf16[1032,128]{1,0:T(8,128)(2,1)S(1)} fusion(bf16[4,128]{1,0:T(4,128)(2,1)S(1)} %convert_bitcast_fusion, bf16[1024,128]{1,0:T(8,128)(2,1)} %bitcast.11), kind=kLoop, calls=%fused_computation.2 | loop fusion | flops 792576 | bytes 527360 | tf_op jit(solution)/shard_map/concatenate | solution.py:354
  6.3 0.7 %collective-permute-start = (bf16[1032,128]{1,0:T(8,128)(2,1)S(1)}, bf16[1032,128]{1,0:T(8,128)(2,1)S(1)}, u32[]{:S(2)}, u32[]{:S(2)}) collective-permute-start(bf16[1032,128]{1,0:T(8,128)(2,1)S(1)} %fusion.1), channel_id=1, source_target_pairs={{0,1},{1,0},{2,3},{3,2},{4,5},{5,4},{6,7},{7,6},{8,9},{9,8},{10,11... | collective-permute-start | bytes 792584 | tf_op jit(solution)/shard_map/ppermute | solution.py:347
  7.0 0.6 %copy-done.11 = s32[16]{0:T(128)S(1)} copy-done((s32[16]{0:T(128)S(1)}, s32[16]{0:T(128)}, u32[]{:S(2)}) %copy-start.11) | copy-done | bytes 88
  7.7 0.1 broadcast_select_fusion
  7.8 8.1 %psum.7.ids = s32[8,16]{1,0:T(8,128)} all-reduce(s32[8,16]{1,0:T(8,128)S(1)} %broadcast_select_fusion), channel_id=1, replica_groups=mesh['snp'=8,'samp'=4] {'snp'}, use_global_device_ids=true, to_apply=%region_0.1 | all-reduce | flops 128 | bytes 1024 | tf_op jit(solution)/shard_map/psum | solution.py:355
  15.8 2.1 %shard_map.59 = bf16[64,512]{1,0:T(8,128)(2,1)} custom-call(s32[8,16]{1,0:T(8,128)} %psum.7.ids, bf16[1024,128]{1,0:T(8,128)(2,1)} %bitcast.12), custom_call_target="tpu_custom_call" | custom-call | tf_op jit(solution)/shard_map/pallas_call | solution.py:323
  17.9 3.4 %all-to-all-start = ((bf16[8,8,512]{2,1,0:T(8,128)(2,1)}), bf16[8,8,512]{2,1,0:T(8,128)(2,1)S(1)}, u32[]{:S(2)}, u32[]{:S(2)}) async-start(bf16[8,8,512]{2,1,0:T(8,128)(2,1)} %bitcast.16), calls=%async_computation | async-start | bytes 131072 | tf_op jit(solution)/shard_map/all_to_all | solution.py:361
  21.3 0.0 collective-permute-done.2.other1
  21.3 0.0 collective-permute-done.own1
  21.4 0.7 %copy-done.1 = bf16[1024,128]{1,0:T(8,128)(2,1)} copy-done((bf16[1024,128]{1,0:T(8,128)(2,1)}, bf16[1024,128]{1,0:T(8,128)(2,1)S(1)}, u32[]{:S(2)}) %copy-start.1) | copy-done | bytes 262168
  22.0 0.1 copy-done.2
  22.1 0.1 copy-done
  22.2 3.2 %shard_map.60 = (s32[72,256]{1,0:T(8,128)}, s32[72,256]{1,0:T(8,128)}, s32[72,256]{1,0:T(8,128)}, s32[72,256]{1,0:T(8,128)}, f32[8,256]{1,0:T(8,128)}) custom-call(bf16[1024,128]{1,0:T(8,128)(2,1)} %bitcast.13, bf16[1032,128]{1,0:T(8,128)(2,1)} %copy-done, bf16[1024,128]{1,0:T(8,128)(2,1)} %copy-done.2, bf16[1024,128]{1,0:T(8,128)(2,1)} %copy-done.1, ...), custom_call_target="tpu_custom_call" | custom-call | tf_op jit(solution)/shard_map/pallas_call | solution.py:323
  25.4 2.6 %collective-permute-start.6 = (s32[72,256]{1,0:T(8,128)}, s32[72,256]{1,0:T(8,128)S(1)}, u32[]{:S(2)}, u32[]{:S(2)}) collective-permute-start(s32[72,256]{1,0:T(8,128)} %get-tuple-element.18), channel_id=1, source_target_pairs={{0,28},{1,25},{2,30},{3,27},{4,0},{5,29},{6,2},{7,31},{8,4},{9,1},... | collective-permute-start | bytes 221192 | tf_op jit(solution)/shard_map/ppermute | solution.py:347
  27.9 6.1 %collective-permute-start.7 = (s32[72,256]{1,0:T(8,128)}, s32[72,256]{1,0:T(8,128)S(1)}, u32[]{:S(2)}, u32[]{:S(2)}) collective-permute-start(s32[72,256]{1,0:T(8,128)} %get-tuple-element.19), channel_id=1, source_target_pairs={{0,29},{1,26},{2,31},{3,24},{4,1},{5,30},{6,3},{7,28},{8,5},{9,2},... | collective-permute-start | bytes 221192 | tf_op jit(solution)/shard_map/ppermute | solution.py:347
  34.0 0.6 %copy-done.3 = bf16[8,8,512]{2,1,0:T(8,128)(2,1)} copy-done((bf16[8,8,512]{2,1,0:T(8,128)(2,1)}, bf16[8,8,512]{2,1,0:T(8,128)(2,1)S(1)}, u32[]{:S(2)}) %copy-start.3) | copy-done | bytes 65560
  34.6 3.7 %shard_map.61 = (s32[88,256]{1,0:T(8,128)}, s32[88,256]{1,0:T(8,128)}, s32[88,256]{1,0:T(8,128)}, s32[88,256]{1,0:T(8,128)}) custom-call(bf16[1024,128]{1,0:T(8,128)(2,1)} %bitcast.14, bf16[1032,128]{1,0:T(8,128)(2,1)} %copy-done, bf16[1024,128]{1,0:T(8,128)(2,1)} %copy-done.2, bf16[1024,128]{1,0:T(8,128)(2,1)} %copy-done.1, s32[1,512]{1,0:T(1,128)} %bitcast.18, ...), custom_call_target="tpu_custom_call" | custom-call | tf_op jit(solution)/shard_map/pallas_call | solution.py:323
  38.3 0.6 %collective-permute-start.3 = (s32[88,256]{1,0:T(8,128)}, s32[88,256]{1,0:T(8,128)S(1)}, u32[]{:S(2)}, u32[]{:S(2)}) collective-permute-start(s32[88,256]{1,0:T(8,128)} %get-tuple-element.15), channel_id=1, source_target_pairs={{0,1},{1,2},{2,3},{3,0},{4,5},{5,6},{6,7},{7,4},{8,9},{9,10},{10,1... | collective-permute-start | bytes 270344 | tf_op jit(solution)/shard_map/ppermute | solution.py:347
  38.9 2.6 %collective-permute-start.4 = (s32[88,256]{1,0:T(8,128)}, s32[88,256]{1,0:T(8,128)S(1)}, u32[]{:S(2)}, u32[]{:S(2)}) collective-permute-start(s32[88,256]{1,0:T(8,128)} %get-tuple-element.16), channel_id=1, source_target_pairs={{0,2},{1,3},{2,0},{3,1},{4,6},{5,7},{6,4},{7,5},{8,10},{9,11},{10,... | collective-permute-start | bytes 270344 | tf_op jit(solution)/shard_map/ppermute | solution.py:347
  41.5 2.4 %collective-permute-start.5 = (s32[88,256]{1,0:T(8,128)}, s32[88,256]{1,0:T(8,128)S(1)}, u32[]{:S(2)}, u32[]{:S(2)}) collective-permute-start(s32[88,256]{1,0:T(8,128)} %get-tuple-element.17), channel_id=1, source_target_pairs={{0,3},{1,0},{2,1},{3,2},{4,7},{5,4},{6,5},{7,6},{8,11},{9,8},{10,9... | collective-permute-start | bytes 270344 | tf_op jit(solution)/shard_map/ppermute | solution.py:347
  43.9 0.1 collective-permute-start.8
  43.9 1.8 %collective-permute-start.9 = (s32[72,256]{1,0:T(8,128)S(1)}, s32[72,256]{1,0:T(8,128)S(1)}, u32[]{:S(2)}, u32[]{:S(2)}) collective-permute-start(s32[72,256]{1,0:T(8,128)S(1)} %copy-done.12), channel_id=1, source_target_pairs={{0,31},{1,24},{2,29},{3,26},{4,3},{5,28},{6,1},{7,30},{8,7},{9,0},... | collective-permute-start | bytes 221192 | tf_op jit(solution)/shard_map/ppermute | solution.py:347
  45.8 7.0 %collective-permute-done.8.a2 = s32[72,256]{1,0:T(8,128)S(1)} collective-permute-done((s32[72,256]{1,0:T(8,128)S(1)}, s32[72,256]{1,0:T(8,128)S(1)}, u32[]{:S(2)}, u32[]{:S(2)}) %collective-permute-start.8) | collective-permute-done | bytes 73760 | tf_op jit(solution)/shard_map/ppermute | solution.py:347
  52.9 0.5 copy-done.9
  53.4 0.0 copy-done.10
  53.5 0.1 copy-done.4
  53.5 0.0 copy-done.5
  53.6 0.0 copy-done.6
  53.6 3.1 %shard_map.62 = (f32[32,4,128]{2,1,0:T(4,128)}, f32[1,16]{1,0:T(1,128)}) custom-call(s32[88,256]{1,0:T(8,128)} %get-tuple-element.14.b0, s32[88,256]{1,0:T(8,128)} %copy-done.4, s32[88,256]{1,0:T(8,128)} %copy-done.5, s32[88,256]{1,0:T(8,128)} %copy-done.6, s32[72,256]{1,0:T(8,128)} %copy-done.7, s32[72,256]{1,0:T(8,128)} %copy-done.8, s32[72,256]{1,0:T(8,128)} %copy-done.9, ...), custom_call_target="tpu_custom_call" | custom-call | tf_op jit(solution)/shard_map/pallas_call | solution.py:323
  (27 shorter events, 0.1 us)
Async XLA Ops:
  0.6 20.7 %collective-permute-start.2 = (bf16[1024,128]{1,0:T(8,128)(2,1)}, bf16[1024,128]{1,0:T(8,128)(2,1)S(1)}, u32[]{:S(2)}, u32[]{:S(2)}) collective-permute-start(bf16[1024,128]{1,0:T(8,128)(2,1)} %bitcast.9), channel_id=1, source_target_pairs={{0,9},{1,4},{2,11},{3,6},{4,13},{5,8},{6,15},{7,10},{8,17},{9,12},... | collective-permute-start | bytes 786440 | tf_op jit(solution)/shard_map/ppermute | solution.py:347
  4.7 16.6 %collective-permute-start.1 = (bf16[1024,128]{1,0:T(8,128)(2,1)}, bf16[1024,128]{1,0:T(8,128)(2,1)S(1)}, u32[]{:S(2)}, u32[]{:S(2)}) collective-permute-start(bf16[1024,128]{1,0:T(8,128)(2,1)} %bitcast.10), channel_id=1, source_target_pairs={{0,4},{1,9},{2,6},{3,11},{4,8},{5,13},{6,10},{7,15},{8,12},{9,17},... | collective-permute-start | bytes 786440 | tf_op jit(solution)/shard_map/ppermute | solution.py:347
  6.3 15.0 %collective-permute-start = (bf16[1032,128]{1,0:T(8,128)(2,1)S(1)}, bf16[1032,128]{1,0:T(8,128)(2,1)S(1)}, u32[]{:S(2)}, u32[]{:S(2)}) collective-permute-start(bf16[1032,128]{1,0:T(8,128)(2,1)S(1)} %fusion.1), channel_id=1, source_target_pairs={{0,1},{1,0},{2,3},{3,2},{4,5},{5,4},{6,7},{7,6},{8,9},{9,8},{10,11... | collective-permute-start | bytes 792584 | tf_op jit(solution)/shard_map/ppermute | solution.py:347
  7.0 0.7 %copy-start.11 = (s32[16]{0:T(128)S(1)}, s32[16]{0:T(128)}, u32[]{:S(2)}) copy-start(s32[16]{0:T(128)} %param.7) | copy-start | bytes 196
  17.9 16.1 %all-to-all-start = ((bf16[8,8,512]{2,1,0:T(8,128)(2,1)}), bf16[8,8,512]{2,1,0:T(8,128)(2,1)S(1)}, u32[]{:S(2)}, u32[]{:S(2)}) async-start(bf16[8,8,512]{2,1,0:T(8,128)(2,1)} %bitcast.16), calls=%async_computation | async-start | bytes 131072 | tf_op jit(solution)/shard_map/all_to_all | solution.py:361
  21.3 0.7 %copy-start.1 = (bf16[1024,128]{1,0:T(8,128)(2,1)}, bf16[1024,128]{1,0:T(8,128)(2,1)S(1)}, u32[]{:S(2)}) copy-start(bf16[1024,128]{1,0:T(8,128)(2,1)S(1)} %collective-permute-done.2.other1) | copy-start | bytes 786436
  21.3 0.8 %copy-start.2 = (bf16[1024,128]{1,0:T(8,128)(2,1)}, bf16[1024,128]{1,0:T(8,128)(2,1)S(1)}, u32[]{:S(2)}) copy-start(bf16[1024,128]{1,0:T(8,128)(2,1)S(1)} %collective-permute-done.1.other0) | copy-start | bytes 786436
  21.3 0.9 %copy-start = (bf16[1032,128]{1,0:T(8,128)(2,1)}, bf16[1032,128]{1,0:T(8,128)(2,1)S(1)}, u32[]{:S(2)}) copy-start(bf16[1032,128]{1,0:T(8,128)(2,1)S(1)} %collective-permute-done.own1) | copy-start | bytes 792580
  25.4 18.5 %collective-permute-start.6 = (s32[72,256]{1,0:T(8,128)}, s32[72,256]{1,0:T(8,128)S(1)}, u32[]{:S(2)}, u32[]{:S(2)}) collective-permute-start(s32[72,256]{1,0:T(8,128)} %get-tuple-element.18), channel_id=1, source_target_pairs={{0,28},{1,25},{2,30},{3,27},{4,0},{5,29},{6,2},{7,31},{8,4},{9,1},... | collective-permute-start | bytes 221192 | tf_op jit(solution)/shard_map/ppermute | solution.py:347
  27.9 16.0 %collective-permute-start.7 = (s32[72,256]{1,0:T(8,128)}, s32[72,256]{1,0:T(8,128)S(1)}, u32[]{:S(2)}, u32[]{:S(2)}) collective-permute-start(s32[72,256]{1,0:T(8,128)} %get-tuple-element.19), channel_id=1, source_target_pairs={{0,29},{1,26},{2,31},{3,24},{4,1},{5,30},{6,3},{7,28},{8,5},{9,2},... | collective-permute-start | bytes 221192 | tf_op jit(solution)/shard_map/ppermute | solution.py:347
  34.0 0.6 %copy-start.3 = (bf16[8,8,512]{2,1,0:T(8,128)(2,1)}, bf16[8,8,512]{2,1,0:T(8,128)(2,1)S(1)}, u32[]{:S(2)}) copy-start(bf16[8,8,512]{2,1,0:T(8,128)(2,1)S(1)} %all-to-all-done) | copy-start | bytes 196612
  34.6 9.2 %copy-start.13 = (s32[72,256]{1,0:T(8,128)S(1)}, s32[72,256]{1,0:T(8,128)}, u32[]{:S(2)}) copy-start(s32[72,256]{1,0:T(8,128)} %get-tuple-element.20) | copy-start | bytes 221188
  34.6 9.3 %copy-start.12 = (s32[72,256]{1,0:T(8,128)S(1)}, s32[72,256]{1,0:T(8,128)}, u32[]{:S(2)}) copy-start(s32[72,256]{1,0:T(8,128)} %get-tuple-element.21) | copy-start | bytes 221188
  38.3 14.5 %collective-permute-start.3 = (s32[88,256]{1,0:T(8,128)}, s32[88,256]{1,0:T(8,128)S(1)}, u32[]{:S(2)}, u32[]{:S(2)}) collective-permute-start(s32[88,256]{1,0:T(8,128)} %get-tuple-element.15), channel_id=1, source_target_pairs={{0,1},{1,2},{2,3},{3,0},{4,5},{5,6},{6,7},{7,4},{8,9},{9,10},{10,1... | collective-permute-start | bytes 270344 | tf_op jit(solution)/shard_map/ppermute | solution.py:347
  38.9 13.9 %collective-permute-start.4 = (s32[88,256]{1,0:T(8,128)}, s32[88,256]{1,0:T(8,128)S(1)}, u32[]{:S(2)}, u32[]{:S(2)}) collective-permute-start(s32[88,256]{1,0:T(8,128)} %get-tuple-element.16), channel_id=1, source_target_pairs={{0,2},{1,3},{2,0},{3,1},{4,6},{5,7},{6,4},{7,5},{8,10},{9,11},{10,... | collective-permute-start | bytes 270344 | tf_op jit(solution)/shard_map/ppermute | solution.py:347
  41.5 11.4 %collective-permute-start.5 = (s32[88,256]{1,0:T(8,128)}, s32[88,256]{1,0:T(8,128)S(1)}, u32[]{:S(2)}, u32[]{:S(2)}) collective-permute-start(s32[88,256]{1,0:T(8,128)} %get-tuple-element.17), channel_id=1, source_target_pairs={{0,3},{1,0},{2,1},{3,2},{4,7},{5,4},{6,5},{7,6},{8,11},{9,8},{10,9... | collective-permute-start | bytes 270344 | tf_op jit(solution)/shard_map/ppermute | solution.py:347
  43.8 9.0 %copy-start.7 = (s32[72,256]{1,0:T(8,128)}, s32[72,256]{1,0:T(8,128)S(1)}, u32[]{:S(2)}) copy-start(s32[72,256]{1,0:T(8,128)S(1)} %collective-permute-done.6.a0) | copy-start | bytes 221188
  43.9 9.0 %collective-permute-start.8 = (s32[72,256]{1,0:T(8,128)S(1)}, s32[72,256]{1,0:T(8,128)S(1)}, u32[]{:S(2)}, u32[]{:S(2)}) collective-permute-start(s32[72,256]{1,0:T(8,128)S(1)} %copy-done.13), channel_id=1, source_target_pairs={{0,30},{1,27},{2,28},{3,25},{4,2},{5,31},{6,0},{7,29},{8,6},{9,3},... | collective-permute-start | bytes 221192 | tf_op jit(solution)/shard_map/ppermute | solution.py:347
  43.9 9.0 %copy-start.8 = (s32[72,256]{1,0:T(8,128)}, s32[72,256]{1,0:T(8,128)S(1)}, u32[]{:S(2)}) copy-start(s32[72,256]{1,0:T(8,128)S(1)} %collective-permute-done.7.a1) | copy-start | bytes 221188
  43.9 8.9 %collective-permute-start.9 = (s32[72,256]{1,0:T(8,128)S(1)}, s32[72,256]{1,0:T(8,128)S(1)}, u32[]{:S(2)}, u32[]{:S(2)}) collective-permute-start(s32[72,256]{1,0:T(8,128)S(1)} %copy-done.12), channel_id=1, source_target_pairs={{0,31},{1,24},{2,29},{3,26},{4,3},{5,28},{6,1},{7,30},{8,7},{9,0},... | collective-permute-start | bytes 221192 | tf_op jit(solution)/shard_map/ppermute | solution.py:347
  52.8 0.6 %copy-start.9 = (s32[72,256]{1,0:T(8,128)}, s32[72,256]{1,0:T(8,128)S(1)}, u32[]{:S(2)}) copy-start(s32[72,256]{1,0:T(8,128)S(1)} %collective-permute-done.8.a2) | copy-start | bytes 221188
  52.8 0.7 %copy-start.10 = (s32[72,256]{1,0:T(8,128)}, s32[72,256]{1,0:T(8,128)S(1)}, u32[]{:S(2)}) copy-start(s32[72,256]{1,0:T(8,128)S(1)} %collective-permute-done.9.a3) | copy-start | bytes 221188
  52.8 0.7 %copy-start.4 = (s32[88,256]{1,0:T(8,128)}, s32[88,256]{1,0:T(8,128)S(1)}, u32[]{:S(2)}) copy-start(s32[88,256]{1,0:T(8,128)S(1)} %collective-permute-done.3.b1) | copy-start | bytes 270340
  52.9 0.7 %copy-start.5 = (s32[88,256]{1,0:T(8,128)}, s32[88,256]{1,0:T(8,128)S(1)}, u32[]{:S(2)}) copy-start(s32[88,256]{1,0:T(8,128)S(1)} %collective-permute-done.4.b2) | copy-start | bytes 270340
  52.9 0.7 %copy-start.6 = (s32[88,256]{1,0:T(8,128)}, s32[88,256]{1,0:T(8,128)S(1)}, u32[]{:S(2)}) copy-start(s32[88,256]{1,0:T(8,128)S(1)} %collective-permute-done.5.b3) | copy-start | bytes 270340

commit v2 on v1

--- a/solution.py
+++ b/solution.py
@@ -104,7 +104,7 @@
             for c in range(2):
                 piece = (turned * classes[c][:, half * samples:(half + 1) * samples]).astype(BF16)
                 for q in range(4):
-                    d = (q + 4 - k) & 3
+                    d = q ^ k
                     left[d, c * 2 + i, :, rows] = piece[q * quarter:(q + 1) * quarter]
         parts = split_genotypes(second_refs[half], wide)
         for j in range(2):
@@ -274,7 +274,7 @@
     for start in range(0, pairs, block):
         count = min(block, pairs - start)
         rows = slice(height + 8 + start, height + 8 + start + count)
-        sums = sum(floating(m[rows, 0:block], 2 * samples) for m in bs[1:]) + floating(b0[rows, 0:block], 2 * samples)
+        sums = floating(b0[rows, 0:block] + b1[rows, 0:block] + b2[rows, 0:block] + b3[rows, 0:block], 2 * samples)
         if count < block:
             sums = jnp.concatenate([sums, jnp.ones((block - count, block), F32)], axis=0)
         turned = sums.T
@@ -319,14 +319,23 @@
     return [pl.BlockSpec(memory_space=pltpu.VMEM)] * count
 
 
-def run(body, args, outs, scratch):
+def run(body, args, outs, scratch, near=True):
     return pl.pallas_call(
         body,
-        out_shape=outs,
+        out_shape=[pltpu.VMEM(o.shape, o.dtype) if near else o for o in outs],
         in_specs=vmem(len(args)),
-        out_specs=jax.tree.map(lambda _: pl.BlockSpec(memory_space=pltpu.VMEM), outs),
+        out_specs=vmem(len(outs)),
         scratch_shapes=scratch,
-    )(*args)
+    )(*(pltpu.with_memory_space_constraint(a, pltpu.VMEM) for a in args))
+
+
+def mark_kernel(geno, label0, out):
+    rows, block = geno.shape
+    out[0:rows, :] = geno[...]
+    case = label0[...].astype(F32)
+    parts = [case[:, q * block:(q + 1) * block] for q in range(case.shape[1] // block)]
+    parts.append(jnp.zeros((out.shape[0] - rows - len(parts), block), F32))
+    out[rows:, :] = jnp.concatenate(parts, axis=0).astype(BF16)
 
 
 def on_device(genotypes, case_labels, refit_own, refit_peer):
@@ -348,15 +357,18 @@
 
     geno = genotypes.reshape(2 * samples, block)
     labels = case_labels.reshape(1, samples)
-    marks = jnp.pad(case_labels.astype(BF16).reshape(samples // block, block), ((0, -(samples // block) % 8), (0, 0)))
+    (marked,) = run(
+        mark_kernel, (geno, labels),
+        [jax.ShapeDtypeStruct((2 * samples + samples // block + -(samples // block) % 8, block), BF16)], [],
+    )
     other0 = moved(geno, lambda b, k: (b + 1 + (k & 1), k))
     other1 = moved(geno, lambda b, k: (b + 2 - (k & 1), k ^ 1))
-    own1 = moved(jnp.concatenate([geno, marks], axis=0), lambda b, k: (b, k ^ 1))
+    own1 = moved(marked, lambda b, k: (b, k ^ 1))
     ids = lax.psum(jnp.where(iota((snp_count, pairs), 0) == here, refit_peer[None, :], 0), "snp")
     wide = pltpu.VMEM((2 * samples, block), F32)
-    sent = run(
+    (sent,) = run(
         functools.partial(select_kernel, shift=shift), (ids, geno),
-        jax.ShapeDtypeStruct((snp_count * 2 * CAP, samples), BF16), [wide],
+        [jax.ShapeDtypeStruct((snp_count * 2 * CAP, samples), BF16)], [wide],
     )
     got = lax.all_to_all(sent, "snp", split_axis=0, concat_axis=0, tiled=True)
     scratch = [wide, pltpu.VMEM((4, 4, block // 4, 2 * samples), BF16), pltpu.VMEM((2 * samples, 2 * block), BF16)]
@@ -367,7 +379,7 @@
         [short] * 4 + [jax.ShapeDtypeStruct((8, 2 * block), F32)], scratch,
     )
     for d in range(4):
-        ahead[d] = moved(ahead[d], lambda b, k: (b - 1 - (k & 1), k + d))
+        ahead[d] = moved(ahead[d], lambda b, k: (b - 1 - (k & 1), k ^ d))
     behind = run(
         functools.partial(behind_kernel, shift=shift),
         (geno, own1, other0, other1, labels, refit_own[None, :], refit_peer[None, :], got, sums),
@@ -375,11 +387,11 @@
     )
     behind = list(behind)
     for d in range(1, 4):
-        behind[d] = moved(behind[d], lambda b, k: (b, k + d))
+        behind[d] = moved(behind[d], lambda b, k: (b, k ^ d))
     screen, stat = run(
         functools.partial(finish_kernel, samples=samples), (*behind, *ahead),
         [jax.ShapeDtypeStruct((block // samp_count, 2 * HALF, block), F32), jax.ShapeDtypeStruct((1, pairs), F32)],
-        [pltpu.VMEM((block, block), F32)],
+        [pltpu.VMEM((block, block), F32)], near=False,
     )
     return screen, stat.reshape(pairs)
 
@@ -387,4 +399,5 @@
 def solution(mesh):
     in_specs = (P("samp", None, "snp"), P("samp"), P("snp"), P("snp"))
     out_specs = (P(("snp", "samp"), None, None), P("snp"))
+
     return jax.shard_map(on_device, mesh=mesh, in_specs=in_specs, out_specs=out_specs, check_vma=False)

time: 57.1 us -> 51.6 us (0.904)
  Pallas kernels: 12 us -> 6.25 us
  waiting for transfers between devices: 7.06 us -> 9.46 us
  other arithmetic: 1.73 us -> 0.08 us
  starting transfers between devices: 24.1 us -> 24.8 us
    pallas_call x4 -> x5, Pallas kernels: 12 us -> 6.25 us  [run(): pl.pallas_call(body, out_shape=[pltpu.VMEM(o.shape, o.dtype) if near else...]
    ppermute x10, waiting for transfers between devices: 7.06 us -> 9.46 us  [moved(): return lax.ppermute(value, ('snp', 'samp'), links)]
    concatenate x1 -> x0, other arithmetic: 0.97 us -> none  [on_device(): jnp.concatenate([geno, marks], axis=0)]
    reshape x1 -> x0, other arithmetic: 0.68 us -> none  [on_device(): case_labels.astype(BF16).reshape(samples // block, block)]
    ppermute x10, starting transfers between devices: 20.8 us -> 21.4 us  [moved(): return lax.ppermute(value, ('snp', 'samp'), links)]
    unnamed x28 -> x8, local copies, waits for them, and re-layouts: 2.82 us -> 2.29 us
  transfers between devices with their start and end apart: 11 -> 11, of which waited for: 1 -> 1; matrix products, arithmetic and copies ran while one was open for 3% -> 0% of each run, Pallas kernels for 16% -> 8%
where the time goes in v2:
time: 51.6 us; the launch traced here: 51.1 us
  starting transfers between devices  24.8 us (48%)
  waiting for transfers between devices  9.46 us (18%)
  blocking collectives  7.55 us (15%)
  Pallas kernels  6.25 us (12%)
  local copies, waits for them, and re-layouts  2.29 us (4%)
  between operations  0.71 us (1%)
    ppermute x10, starting transfers between devices, moved(): return lax.ppermute(value, ('snp', 'samp'), links)  21.4 us
    ppermute x10, waiting for transfers between devices, moved(): return lax.ppermute(value, ('snp', 'samp'), links)  9.46 us
    psum x1, blocking collectives, on_device(): lax.psum(jnp.where(iota((snp_count, pairs), 0) == here, refit_peer[None,...  7.55 us
    pallas_call x5, Pallas kernels, run(): pl.pallas_call(body, out_shape=[pltpu.VMEM(o.shape, o.dtype) if near else...  6.25 us
    all_to_all x1, starting transfers between devices, on_device(): got = lax.all_to_all(sent, 'snp', split_axis=0, concat_axis=0, tiled=True)  3.35 us
    unnamed x8, local copies, waits for them, and re-layouts  2.29 us
  transfers between devices with their start and end apart: 11, of which 1 were waited for; matrix products, arithmetic and copies ran while one was open for 0% of the time, Pallas kernels for 8%

profile of v2, /device:TPU:0, one launch (start us, length us, event | category | flops | bytes accessed | tf_op | source)
XLA Modules:
  0.0 51.1 jit_solution(15588251399142795552)
XLA Ops:
  0.6 0.0 copy-start.1
  0.6 4.0 %collective-permute-start.2 = (bf16[1024,128]{1,0:T(8,128)(2,1)}, bf16[1024,128]{1,0:T(8,128)(2,1)S(1)}, u32[]{:S(2)}, u32[]{:S(2)}) collective-permute-start(bf16[1024,128]{1,0:T(8,128)(2,1)} %bitcast.7), channel_id=1, source_target_pairs={{0,9},{1,4},{2,11},{3,6},{4,13},{5,8},{6,15},{7,10},{8,17},{9,12},... | collective-permute-start | bytes 786440 | tf_op jit(solution)/shard_map/ppermute | solution.py:356
  4.7 0.0 collective-permute-start.1
  4.7 1.0 %copy-done = bf16[512,2,128]{2,1,0:T(2,128)(2,1)S(1)} copy-done((bf16[512,2,128]{2,1,0:T(2,128)(2,1)S(1)}, bf16[512,2,128]{2,1,0:T(2,128)(2,1)}, u32[]{:S(2)}) %copy-start) | copy-done | bytes 262168
  5.7 0.7 %collective-permute-start = (bf16[1032,128]{1,0:T(8,128)(2,1)S(1)}, bf16[1032,128]{1,0:T(8,128)(2,1)S(1)}, u32[]{:S(2)}, u32[]{:S(2)}) collective-permute-start(bf16[1032,128]{1,0:T(8,128)(2,1)S(1)} %shard_map.59), channel_id=1, source_target_pairs={{0,1},{1,0},{2,3},{3,2},{4,5},{5,4},{6,7},{7,6},{8,9},{9,8},{10,11... | collective-permute-start | bytes 792584 | tf_op jit(solution)/shard_map/ppermute | solution.py:356
  6.4 0.6 %copy-done.2 = s32[16]{0:T(128)S(1)} copy-done((s32[16]{0:T(128)S(1)}, s32[16]{0:T(128)}, u32[]{:S(2)}) %copy-start.2) | copy-done | bytes 88
  7.0 0.1 broadcast_select_fusion
  7.1 7.6 %psum.7.ids = s32[8,16]{1,0:T(8,128)S(1)} all-reduce(s32[8,16]{1,0:T(8,128)S(1)} %broadcast_select_fusion), channel_id=1, replica_groups=mesh['snp'=8,'samp'=4] {'snp'}, use_global_device_ids=true, to_apply=%region_0.1 | all-reduce | flops 128 | bytes 1024 | tf_op jit(solution)/shard_map/psum | solution.py:367
  14.7 1.1 %shard_map.60 = bf16[64,512]{1,0:T(8,128)(2,1)} custom-call(s32[8,16]{1,0:T(8,128)S(1)} %psum.7.ids, bf16[1024,128]{1,0:T(8,128)(2,1)S(1)} %bitcast.10), custom_call_target="tpu_custom_call" | custom-call | tf_op jit(solution)/shard_map/pallas_call | solution.py:323
  15.8 3.4 %all-to-all-start = ((bf16[8,8,512]{2,1,0:T(8,128)(2,1)}), bf16[8,8,512]{2,1,0:T(8,128)(2,1)S(1)}, u32[]{:S(2)}, u32[]{:S(2)}) async-start(bf16[8,8,512]{2,1,0:T(8,128)(2,1)} %bitcast.4), calls=%async_computation | async-start | bytes 131072 | tf_op jit(solution)/shard_map/all_to_all | solution.py:373
  19.2 0.0 collective-permute-done.2.other1
  19.2 0.0 collective-permute-done.1.other0
  19.2 0.0 collective-permute-done.own1
  19.2 1.4 %shard_map.61 = (s32[72,256]{1,0:T(8,128)S(1)}, s32[72,256]{1,0:T(8,128)S(1)}, s32[72,256]{1,0:T(8,128)S(1)}, s32[72,256]{1,0:T(8,128)S(1)}, f32[8,256]{1,0:T(8,128)S(1)}) custom-call(bf16[1024,128]{1,0:T(8,128)(2,1)S(1)} %bitcast.11, bf16[1032,128]{1,0:T(8,128)(2,1)S(1)} %collective-permute-done.own1, bf16[1024,128]{1,0:T(8,128)(2,1)S(1)} %collective-permute-done.1.other0, ...), custom_call_target="tpu_custom_call" | custom-call | tf_op jit(solution)/shard_map/pallas_call | solution.py:323
  20.6 2.6 %collective-permute-start.6 = (s32[72,256]{1,0:T(8,128)S(1)}, s32[72,256]{1,0:T(8,128)S(1)}, u32[]{:S(2)}, u32[]{:S(2)}) collective-permute-start(s32[72,256]{1,0:T(8,128)S(1)} %get-tuple-element.18), channel_id=1, source_target_pairs={{0,28},{1,25},{2,30},{3,27},{4,0},{5,29},{6,2},{7,31},{8,4},{9,1},... | collective-permute-start | bytes 221192 | tf_op jit(solution)/shard_map/ppermute | solution.py:356
  23.2 6.7 %collective-permute-start.7 = (s32[72,256]{1,0:T(8,128)S(1)}, s32[72,256]{1,0:T(8,128)S(1)}, u32[]{:S(2)}, u32[]{:S(2)}) collective-permute-start(s32[72,256]{1,0:T(8,128)S(1)} %get-tuple-element.19), channel_id=1, source_target_pairs={{0,29},{1,24},{2,31},{3,26},{4,1},{5,28},{6,3},{7,30},{8,5},{9,0},... | collective-permute-start | bytes 221192 | tf_op jit(solution)/shard_map/ppermute | solution.py:356
  29.9 0.0 all-to-all-done
  29.9 0.7 %copy-done.3 = s32[16]{0:T(128)S(1)} copy-done((s32[16]{0:T(128)S(1)}, s32[16]{0:T(128)}, u32[]{:S(2)}) %copy-start.3) | copy-done | bytes 88
  30.5 1.8 %shard_map.62 = (s32[88,256]{1,0:T(8,128)S(1)}, s32[88,256]{1,0:T(8,128)S(1)}, s32[88,256]{1,0:T(8,128)S(1)}, s32[88,256]{1,0:T(8,128)S(1)}) custom-call(bf16[1024,128]{1,0:T(8,128)(2,1)S(1)} %bitcast.12, bf16[1032,128]{1,0:T(8,128)(2,1)S(1)} %collective-permute-done.own1, bf16[1024,128]{1,0:T(8,128)(2,1)S(1)} %collective-permute-done.1.other0, ...), custom_call_target="tpu_custom_call" | custom-call | tf_op jit(solution)/shard_map/pallas_call | solution.py:323
  32.3 1.3 %collective-permute-start.3 = (s32[88,256]{1,0:T(8,128)S(1)}, s32[88,256]{1,0:T(8,128)S(1)}, u32[]{:S(2)}, u32[]{:S(2)}) collective-permute-start(s32[88,256]{1,0:T(8,128)S(1)} %get-tuple-element.15), channel_id=1, source_target_pairs={{0,1},{1,0},{2,3},{3,2},{4,5},{5,4},{6,7},{7,6},{8,9},{9,8},{10,11... | collective-permute-start | bytes 270344 | tf_op jit(solution)/shard_map/ppermute | solution.py:356
  33.6 2.6 %collective-permute-start.4 = (s32[88,256]{1,0:T(8,128)S(1)}, s32[88,256]{1,0:T(8,128)S(1)}, u32[]{:S(2)}, u32[]{:S(2)}) collective-permute-start(s32[88,256]{1,0:T(8,128)S(1)} %get-tuple-element.16), channel_id=1, source_target_pairs={{0,2},{1,3},{2,0},{3,1},{4,6},{5,7},{6,4},{7,5},{8,10},{9,11},{10,... | collective-permute-start | bytes 270344 | tf_op jit(solution)/shard_map/ppermute | solution.py:356
  36.2 0.6 %collective-permute-start.5 = (s32[88,256]{1,0:T(8,128)S(1)}, s32[88,256]{1,0:T(8,128)S(1)}, u32[]{:S(2)}, u32[]{:S(2)}) collective-permute-start(s32[88,256]{1,0:T(8,128)S(1)} %get-tuple-element.17), channel_id=1, source_target_pairs={{0,3},{1,2},{2,1},{3,0},{4,7},{5,6},{6,5},{7,4},{8,11},{9,10},{10,... | collective-permute-start | bytes 270344 | tf_op jit(solution)/shard_map/ppermute | solution.py:356
  36.8 0.0 collective-permute-done.6.a0
  36.8 1.1 %collective-permute-start.8 = (s32[72,256]{1,0:T(8,128)S(1)}, s32[72,256]{1,0:T(8,128)S(1)}, u32[]{:S(2)}, u32[]{:S(2)}) collective-permute-start(s32[72,256]{1,0:T(8,128)S(1)} %get-tuple-element.20), channel_id=1, source_target_pairs={{0,30},{1,27},{2,28},{3,25},{4,2},{5,31},{6,0},{7,29},{8,6},{9,3},... | collective-permute-start | bytes 221192 | tf_op jit(solution)/shard_map/ppermute | solution.py:356
  37.9 0.0 collective-permute-done.7.a1
  37.9 1.8 %collective-permute-start.9 = (s32[72,256]{1,0:T(8,128)S(1)}, s32[72,256]{1,0:T(8,128)S(1)}, u32[]{:S(2)}, u32[]{:S(2)}) collective-permute-start(s32[72,256]{1,0:T(8,128)S(1)} %get-tuple-element.21), channel_id=1, source_target_pairs={{0,31},{1,26},{2,29},{3,24},{4,3},{5,30},{6,1},{7,28},{8,7},{9,2},... | collective-permute-start | bytes 221192 | tf_op jit(solution)/shard_map/ppermute | solution.py:356
  39.7 9.4 %collective-permute-done.8.a2 = s32[72,256]{1,0:T(8,128)S(1)} collective-permute-done((s32[72,256]{1,0:T(8,128)S(1)}, s32[72,256]{1,0:T(8,128)S(1)}, u32[]{:S(2)}, u32[]{:S(2)}) %collective-permute-start.8) | collective-permute-done | bytes 73760 | tf_op jit(solution)/shard_map/ppermute | solution.py:356
  49.1 0.0 collective-permute-done.9.a3
  49.1 0.0 collective-permute-done.3.b1
  49.1 0.0 collective-permute-done.4.b2
  49.1 0.0 collective-permute-done.5.b3
  49.1 1.9 %shard_map.63 = (f32[32,4,128]{2,1,0:T(4,128)}, f32[1,16]{1,0:T(1,128)}) custom-call(s32[88,256]{1,0:T(8,128)S(1)} %get-tuple-element.14.b0, s32[88,256]{1,0:T(8,128)S(1)} %collective-permute-done.3.b1, s32[88,256]{1,0:T(8,128)S(1)} %collective-permute-done.4.b2, s32[88,256]{1,0:T(8,128)S(1)} %collective-permute-done.5.b3, ...), custom_call_target="tpu_custom_call" | custom-call | tf_op jit(solution)/shard_map/pallas_call | solution.py:323
  (6 shorter events, 0.0 us)
Async XLA Ops:
  0.6 4.1 %copy-start.1 = (s32[512]{0:T(512)S(1)}, s32[512]{0:T(512)}, u32[]{:S(2)}) copy-start(s32[512]{0:T(512)} %param.5) | copy-start | bytes 6148
  0.6 18.5 %collective-permute-start.2 = (bf16[1024,128]{1,0:T(8,128)(2,1)}, bf16[1024,128]{1,0:T(8,128)(2,1)S(1)}, u32[]{:S(2)}, u32[]{:S(2)}) collective-permute-start(bf16[1024,128]{1,0:T(8,128)(2,1)} %bitcast.7), channel_id=1, source_target_pairs={{0,9},{1,4},{2,11},{3,6},{4,13},{5,8},{6,15},{7,10},{8,17},{9,12},... | collective-permute-start | bytes 786440 | tf_op jit(solution)/shard_map/ppermute | solution.py:356
  4.7 14.5 %collective-permute-start.1 = (bf16[1024,128]{1,0:T(8,128)(2,1)}, bf16[1024,128]{1,0:T(8,128)(2,1)S(1)}, u32[]{:S(2)}, u32[]{:S(2)}) collective-permute-start(bf16[1024,128]{1,0:T(8,128)(2,1)} %bitcast.8), channel_id=1, source_target_pairs={{0,4},{1,9},{2,6},{3,11},{4,8},{5,13},{6,10},{7,15},{8,12},{9,17},... | collective-permute-start | bytes 786440 | tf_op jit(solution)/shard_map/ppermute | solution.py:356
  4.7 1.0 %copy-start = (bf16[512,2,128]{2,1,0:T(2,128)(2,1)S(1)}, bf16[512,2,128]{2,1,0:T(2,128)(2,1)}, u32[]{:S(2)}) copy-start(bf16[512,2,128]{2,1,0:T(2,128)(2,1)} %param.4) | copy-start | bytes 786436
  5.7 13.5 %collective-permute-start = (bf16[1032,128]{1,0:T(8,128)(2,1)S(1)}, bf16[1032,128]{1,0:T(8,128)(2,1)S(1)}, u32[]{:S(2)}, u32[]{:S(2)}) collective-permute-start(bf16[1032,128]{1,0:T(8,128)(2,1)S(1)} %shard_map.59), channel_id=1, source_target_pairs={{0,1},{1,0},{2,3},{3,2},{4,5},{5,4},{6,7},{7,6},{8,9},{9,8},{10,11... | collective-permute-start | bytes 792584 | tf_op jit(solution)/shard_map/ppermute | solution.py:356
  6.4 0.7 %copy-start.2 = (s32[16]{0:T(128)S(1)}, s32[16]{0:T(128)}, u32[]{:S(2)}) copy-start(s32[16]{0:T(128)} %param.7) | copy-start | bytes 196
  15.8 14.1 %all-to-all-start = ((bf16[8,8,512]{2,1,0:T(8,128)(2,1)}), bf16[8,8,512]{2,1,0:T(8,128)(2,1)S(1)}, u32[]{:S(2)}, u32[]{:S(2)}) async-start(bf16[8,8,512]{2,1,0:T(8,128)(2,1)} %bitcast.4), calls=%async_computation | async-start | bytes 131072 | tf_op jit(solution)/shard_map/all_to_all | solution.py:373
  20.6 16.2 %collective-permute-start.6 = (s32[72,256]{1,0:T(8,128)S(1)}, s32[72,256]{1,0:T(8,128)S(1)}, u32[]{:S(2)}, u32[]{:S(2)}) collective-permute-start(s32[72,256]{1,0:T(8,128)S(1)} %get-tuple-element.18), channel_id=1, source_target_pairs={{0,28},{1,25},{2,30},{3,27},{4,0},{5,29},{6,2},{7,31},{8,4},{9,1},... | collective-permute-start | bytes 221192 | tf_op jit(solution)/shard_map/ppermute | solution.py:356
  23.2 14.7 %collective-permute-start.7 = (s32[72,256]{1,0:T(8,128)S(1)}, s32[72,256]{1,0:T(8,128)S(1)}, u32[]{:S(2)}, u32[]{:S(2)}) collective-permute-start(s32[72,256]{1,0:T(8,128)S(1)} %get-tuple-element.19), channel_id=1, source_target_pairs={{0,29},{1,24},{2,31},{3,26},{4,1},{5,28},{6,3},{7,30},{8,5},{9,0},... | collective-permute-start | bytes 221192 | tf_op jit(solution)/shard_map/ppermute | solution.py:356
  29.9 0.7 %copy-start.3 = (s32[16]{0:T(128)S(1)}, s32[16]{0:T(128)}, u32[]{:S(2)}) copy-start(s32[16]{0:T(128)} %param.6) | copy-start | bytes 196
  32.3 16.8 %collective-permute-start.3 = (s32[88,256]{1,0:T(8,128)S(1)}, s32[88,256]{1,0:T(8,128)S(1)}, u32[]{:S(2)}, u32[]{:S(2)}) collective-permute-start(s32[88,256]{1,0:T(8,128)S(1)} %get-tuple-element.15), channel_id=1, source_target_pairs={{0,1},{1,0},{2,3},{3,2},{4,5},{5,4},{6,7},{7,6},{8,9},{9,8},{10,11... | collective-permute-start | bytes 270344 | tf_op jit(solution)/shard_map/ppermute | solution.py:356
  33.6 15.6 %collective-permute-start.4 = (s32[88,256]{1,0:T(8,128)S(1)}, s32[88,256]{1,0:T(8,128)S(1)}, u32[]{:S(2)}, u32[]{:S(2)}) collective-permute-start(s32[88,256]{1,0:T(8,128)S(1)} %get-tuple-element.16), channel_id=1, source_target_pairs={{0,2},{1,3},{2,0},{3,1},{4,6},{5,7},{6,4},{7,5},{8,10},{9,11},{10,... | collective-permute-start | bytes 270344 | tf_op jit(solution)/shard_map/ppermute | solution.py:356
  36.2 13.0 %collective-permute-start.5 = (s32[88,256]{1,0:T(8,128)S(1)}, s32[88,256]{1,0:T(8,128)S(1)}, u32[]{:S(2)}, u32[]{:S(2)}) collective-permute-start(s32[88,256]{1,0:T(8,128)S(1)} %get-tuple-element.17), channel_id=1, source_target_pairs={{0,3},{1,2},{2,1},{3,0},{4,7},{5,6},{6,5},{7,4},{8,11},{9,10},{10,... | collective-permute-start | bytes 270344 | tf_op jit(solution)/shard_map/ppermute | solution.py:356
  36.8 12.4 %collective-permute-start.8 = (s32[72,256]{1,0:T(8,128)S(1)}, s32[72,256]{1,0:T(8,128)S(1)}, u32[]{:S(2)}, u32[]{:S(2)}) collective-permute-start(s32[72,256]{1,0:T(8,128)S(1)} %get-tuple-element.20), channel_id=1, source_target_pairs={{0,30},{1,27},{2,28},{3,25},{4,2},{5,31},{6,0},{7,29},{8,6},{9,3},... | collective-permute-start | bytes 221192 | tf_op jit(solution)/shard_map/ppermute | solution.py:356
  37.9 11.2 %collective-permute-start.9 = (s32[72,256]{1,0:T(8,128)S(1)}, s32[72,256]{1,0:T(8,128)S(1)}, u32[]{:S(2)}, u32[]{:S(2)}) collective-permute-start(s32[72,256]{1,0:T(8,128)S(1)} %get-tuple-element.21), channel_id=1, source_target_pairs={{0,31},{1,26},{2,29},{3,24},{4,3},{5,30},{6,1},{7,28},{8,7},{9,2},... | collective-permute-start | bytes 221192 | tf_op jit(solution)/shard_map/ppermute | solution.py:356

commit v3 on v2

--- a/solution.py
+++ b/solution.py
@@ -329,13 +329,22 @@
     )(*(pltpu.with_memory_space_constraint(a, pltpu.VMEM) for a in args))
 
 
-def mark_kernel(geno, label0, out):
+def stage_kernel(geno, label0, own_ids, peer_ids, out, label_copy, own_copy, peer_copy, placed, sems):
     rows, block = geno.shape
-    out[0:rows, :] = geno[...]
-    case = label0[...].astype(F32)
+    copies = [
+        pltpu.make_async_copy(src, dst, sems.at[n])
+        for n, (src, dst) in enumerate(((geno, out.at[0:rows]), (label0, label_copy), (own_ids, own_copy), (peer_ids, peer_copy)))
+    ]
+    for copy in copies:
+        copy.start()
+    for copy in copies[1:]:
+        copy.wait()
+    placed[...] = jnp.where(iota(placed.shape, 0) == lax.axis_index("snp"), peer_copy[...], 0)
+    case = label_copy[...].astype(F32)
     parts = [case[:, q * block:(q + 1) * block] for q in range(case.shape[1] // block)]
     parts.append(jnp.zeros((out.shape[0] - rows - len(parts), block), F32))
     out[rows:, :] = jnp.concatenate(parts, axis=0).astype(BF16)
+    copies[0].wait()
 
 
 def on_device(genotypes, case_labels, refit_own, refit_peer):
@@ -345,7 +354,6 @@
     samp_count = lax.axis_size("samp")
     assert samp_count == 2 * HALF and block & (block - 1) == 0
     shift = block.bit_length() - 1
-    here = lax.axis_index("snp")
 
     def moved(value, where):
         links = []
@@ -357,17 +365,23 @@
 
     geno = genotypes.reshape(2 * samples, block)
     labels = case_labels.reshape(1, samples)
-    (marked,) = run(
-        mark_kernel, (geno, labels),
-        [jax.ShapeDtypeStruct((2 * samples + samples // block + -(samples // block) % 8, block), BF16)], [],
-    )
+    row_of = lambda count: pltpu.VMEM((1, count), jnp.int32)
+    height = 2 * samples + samples // block + -(samples // block) % 8
+    marked, labels, own_ids, peer_ids, placed = pl.pallas_call(
+        stage_kernel,
+        out_shape=[pltpu.VMEM((height, block), BF16), row_of(samples), row_of(pairs), row_of(pairs),
+                   pltpu.VMEM((snp_count, pairs), jnp.int32)],
+        in_specs=[pl.BlockSpec(memory_space=pl.ANY)] * 4,
+        out_specs=vmem(5),
+        scratch_shapes=[pltpu.SemaphoreType.DMA((4,))],
+    )(geno, labels, refit_own[None, :], refit_peer[None, :])
     other0 = moved(geno, lambda b, k: (b + 1 + (k & 1), k))
     other1 = moved(geno, lambda b, k: (b + 2 - (k & 1), k ^ 1))
     own1 = moved(marked, lambda b, k: (b, k ^ 1))
-    ids = lax.psum(jnp.where(iota((snp_count, pairs), 0) == here, refit_peer[None, :], 0), "snp")
+    ids = lax.psum(placed, "snp")
     wide = pltpu.VMEM((2 * samples, block), F32)
     (sent,) = run(
-        functools.partial(select_kernel, shift=shift), (ids, geno),
+        functools.partial(select_kernel, shift=shift), (ids, marked),
         [jax.ShapeDtypeStruct((snp_count * 2 * CAP, samples), BF16)], [wide],
     )
     got = lax.all_to_all(sent, "snp", split_axis=0, concat_axis=0, tiled=True)
@@ -375,14 +389,14 @@
     short = jax.ShapeDtypeStruct((block // 2 + 8, 2 * block), jnp.int32)
     tall = jax.ShapeDtypeStruct((block // 2 + 8 + pairs, 2 * block), jnp.int32)
     *ahead, sums = run(
-        ahead_kernel, (geno, own1, other0, other1, labels),
+        ahead_kernel, (marked, own1, other0, other1, labels),
         [short] * 4 + [jax.ShapeDtypeStruct((8, 2 * block), F32)], scratch,
     )
     for d in range(4):
         ahead[d] = moved(ahead[d], lambda b, k: (b - 1 - (k & 1), k ^ d))
     behind = run(
         functools.partial(behind_kernel, shift=shift),
-        (geno, own1, other0, other1, labels, refit_own[None, :], refit_peer[None, :], got, sums),
+        (marked, own1, other0, other1, labels, own_ids, peer_ids, got, sums),
         [tall] * 4, scratch,
     )
     behind = list(behind)

time: 51.6 us -> 52.7 us (1.021)
  local copies, waits for them, and re-layouts: 2.29 us -> 0.01 us
  starting transfers between devices: 24.8 us -> 26.5 us
  Pallas kernels: 6.25 us -> 7.24 us
  blocking collectives: 7.55 us -> 8.27 us
    unnamed x8 -> x2, local copies, waits for them, and re-layouts: 2.29 us -> 0.01 us
    all_to_all x1, starting transfers between devices: 3.35 us -> 4.57 us  [on_device(): got = lax.all_to_all(sent, 'snp', split_axis=0, concat_axis=0, tiled=True)]
    pallas_call x0 -> x1, Pallas kernels: none -> 1.05 us  [on_device(): pl.pallas_call(stage_kernel, out_shape=[pltpu.VMEM((height, block), BF16)...]
    psum x1, blocking collectives: 7.55 us -> 8.27 us  [on_device(): ids = lax.psum(placed, 'snp')]
    ppermute x10, starting transfers between devices: 21.4 us -> 22 us  [moved(): return lax.ppermute(value, ('snp', 'samp'), links)]
    pallas_call x5 -> x4, Pallas kernels: 6.25 us -> 6.19 us  [run(): pl.pallas_call(body, out_shape=[pltpu.VMEM(o.shape, o.dtype) if near else...]
where the time goes in v3:
time: 52.7 us; the launch traced here: 52.2 us
  starting transfers between devices  26.5 us (50%)
  waiting for transfers between devices  9.42 us (18%)
  blocking collectives  8.27 us (16%)
  Pallas kernels  7.24 us (14%)
  between operations  0.7 us (1%)
    ppermute x10, starting transfers between devices, moved(): return lax.ppermute(value, ('snp', 'samp'), links)  22 us
    ppermute x10, waiting for transfers between devices, moved(): return lax.ppermute(value, ('snp', 'samp'), links)  9.41 us
    psum x1, blocking collectives, on_device(): ids = lax.psum(placed, 'snp')  8.27 us
    pallas_call x4, Pallas kernels, run(): pl.pallas_call(body, out_shape=[pltpu.VMEM(o.shape, o.dtype) if near else...  6.19 us
    all_to_all x1, starting transfers between devices, on_device(): got = lax.all_to_all(sent, 'snp', split_axis=0, concat_axis=0, tiled=True)  4.57 us
  transfers between devices with their start and end apart: 11, of which 1 were waited for; matrix products, arithmetic and copies ran while one was open for 0% of the time, Pallas kernels for 8%

profile of v3, /device:TPU:0, one launch (start us, length us, event | category | flops | bytes accessed | tf_op | source)
XLA Modules:
  0.0 52.2 jit_solution(1233455153683288443)
XLA Ops:
  0.6 0.0 copy-start
  0.6 1.1 %shard_map.59 = (bf16[1032,128]{1,0:T(8,128)(2,1)S(1)}, s32[1,512]{1,0:T(1,128)S(1)}, s32[1,16]{1,0:T(1,128)S(1)}, s32[1,16]{1,0:T(1,128)S(1)}, s32[8,16]{1,0:T(8,128)S(1)}) custom-call(bf16[1024,128]{1,0:T(8,128)(2,1)} %bitcast.8, s32[1,512]{1,0:T(1,128)} %bitcast.11, s32[1,16]{1,0:T(1,128)} %bitcast.12, s32[1,16]{1,0:T(1,128)} %bitcast.13), custom_call_target="tpu_custom_call" | custom-call | tf_op jit(solution)/shard_map/pallas_call | solution.py:370
  1.7 3.1 %collective-permute-start = (bf16[1032,128]{1,0:T(8,128)(2,1)S(1)}, bf16[1032,128]{1,0:T(8,128)(2,1)S(1)}, u32[]{:S(2)}, u32[]{:S(2)}) collective-permute-start(bf16[1032,128]{1,0:T(8,128)(2,1)S(1)} %get-tuple-element.18.geno.own0), channel_id=1, source_target_pairs={{0,1},{1,0},{2,3},{3,2},{4,5},{5,4},{6,7},{7,6},{8,9},{9,8},{10,11... | collective-permute-start | bytes 792584 | tf_op jit(solution)/shard_map/ppermute | solution.py:364
  4.8 0.0 copy-done
  4.8 1.4 %collective-permute-start.2 = (bf16[1024,128]{1,0:T(8,128)(2,1)S(1)}, bf16[1024,128]{1,0:T(8,128)(2,1)S(1)}, u32[]{:S(2)}, u32[]{:S(2)}) collective-permute-start(bf16[1024,128]{1,0:T(8,128)(2,1)S(1)} %bitcast.9), channel_id=1, source_target_pairs={{0,9},{1,4},{2,11},{3,6},{4,13},{5,8},{6,15},{7,10},{8,17},{9,12},... | collective-permute-start | bytes 786440 | tf_op jit(solution)/shard_map/ppermute | solution.py:364
  6.2 0.0 collective-permute-start.1
  6.2 8.3 %psum.7.ids = s32[8,16]{1,0:T(8,128)S(1)} all-reduce(s32[8,16]{1,0:T(8,128)S(1)} %get-tuple-element.22), channel_id=1, replica_groups=mesh['snp'=8,'samp'=4] {'snp'}, use_global_device_ids=true, to_apply=%region_0.0 | all-reduce | flops 128 | bytes 1024 | tf_op jit(solution)/shard_map/psum | solution.py:381
  14.5 1.1 %shard_map.60 = bf16[64,512]{1,0:T(8,128)(2,1)} custom-call(s32[8,16]{1,0:T(8,128)S(1)} %psum.7.ids, bf16[1032,128]{1,0:T(8,128)(2,1)S(1)} %get-tuple-element.18.geno.own0), custom_call_target="tpu_custom_call" | custom-call | tf_op jit(solution)/shard_map/pallas_call | solution.py:323
  15.6 4.6 %all-to-all-start = ((bf16[8,8,512]{2,1,0:T(8,128)(2,1)}), bf16[8,8,512]{2,1,0:T(8,128)(2,1)S(1)}, u32[]{:S(2)}, u32[]{:S(2)}) async-start(bf16[8,8,512]{2,1,0:T(8,128)(2,1)} %bitcast.4), calls=%async_computation | async-start | bytes 131072 | tf_op jit(solution)/shard_map/all_to_all | solution.py:387
  20.2 0.0 collective-permute-done.2.other1
  20.2 0.0 collective-permute-done.1.other0
  20.2 0.0 collective-permute-done.own1
  20.2 1.4 %shard_map.61 = (s32[72,256]{1,0:T(8,128)S(1)}, s32[72,256]{1,0:T(8,128)S(1)}, s32[72,256]{1,0:T(8,128)S(1)}, s32[72,256]{1,0:T(8,128)S(1)}, f32[8,256]{1,0:T(8,128)S(1)}) custom-call(bf16[1032,128]{1,0:T(8,128)(2,1)S(1)} %get-tuple-element.18.geno.own0, bf16[1032,128]{1,0:T(8,128)(2,1)S(1)} %collective-permute-done.own1, ...), custom_call_target="tpu_custom_call" | custom-call | tf_op jit(solution)/shard_map/pallas_call | solution.py:323
  21.6 2.7 %collective-permute-start.6 = (s32[72,256]{1,0:T(8,128)S(1)}, s32[72,256]{1,0:T(8,128)S(1)}, u32[]{:S(2)}, u32[]{:S(2)}) collective-permute-start(s32[72,256]{1,0:T(8,128)S(1)} %get-tuple-element.28), channel_id=1, source_target_pairs={{0,28},{1,25},{2,30},{3,27},{4,0},{5,29},{6,2},{7,31},{8,4},{9,1},... | collective-permute-start | bytes 221192 | tf_op jit(solution)/shard_map/ppermute | solution.py:364
  24.3 7.4 %collective-permute-start.7 = (s32[72,256]{1,0:T(8,128)S(1)}, s32[72,256]{1,0:T(8,128)S(1)}, u32[]{:S(2)}, u32[]{:S(2)}) collective-permute-start(s32[72,256]{1,0:T(8,128)S(1)} %get-tuple-element.29), channel_id=1, source_target_pairs={{0,29},{1,24},{2,31},{3,26},{4,1},{5,28},{6,3},{7,30},{8,5},{9,0},... | collective-permute-start | bytes 221192 | tf_op jit(solution)/shard_map/ppermute | solution.py:364
  31.6 0.0 all-to-all-done
  31.6 1.8 %shard_map.62 = (s32[88,256]{1,0:T(8,128)S(1)}, s32[88,256]{1,0:T(8,128)S(1)}, s32[88,256]{1,0:T(8,128)S(1)}, s32[88,256]{1,0:T(8,128)S(1)}) custom-call(bf16[1032,128]{1,0:T(8,128)(2,1)S(1)} %get-tuple-element.18.geno.own0, bf16[1032,128]{1,0:T(8,128)(2,1)S(1)} %collective-permute-done.own1, bf16[1024,128]{1,0:T(8,128)(2,1)S(1)} %collective-permute-done.1.other0, ...), custom_call_target="tpu_custom_call" | custom-call | tf_op jit(solution)/shard_map/pallas_call | solution.py:323
  33.4 1.3 %collective-permute-start.3 = (s32[88,256]{1,0:T(8,128)S(1)}, s32[88,256]{1,0:T(8,128)S(1)}, u32[]{:S(2)}, u32[]{:S(2)}) collective-permute-start(s32[88,256]{1,0:T(8,128)S(1)} %get-tuple-element.25), channel_id=1, source_target_pairs={{0,1},{1,0},{2,3},{3,2},{4,5},{5,4},{6,7},{7,6},{8,9},{9,8},{10,11... | collective-permute-start | bytes 270344 | tf_op jit(solution)/shard_map/ppermute | solution.py:364
  34.7 2.6 %collective-permute-start.4 = (s32[88,256]{1,0:T(8,128)S(1)}, s32[88,256]{1,0:T(8,128)S(1)}, u32[]{:S(2)}, u32[]{:S(2)}) collective-permute-start(s32[88,256]{1,0:T(8,128)S(1)} %get-tuple-element.26), channel_id=1, source_target_pairs={{0,2},{1,3},{2,0},{3,1},{4,6},{5,7},{6,4},{7,5},{8,10},{9,11},{10,... | collective-permute-start | bytes 270344 | tf_op jit(solution)/shard_map/ppermute | solution.py:364
  37.2 0.6 %collective-permute-start.5 = (s32[88,256]{1,0:T(8,128)S(1)}, s32[88,256]{1,0:T(8,128)S(1)}, u32[]{:S(2)}, u32[]{:S(2)}) collective-permute-start(s32[88,256]{1,0:T(8,128)S(1)} %get-tuple-element.27), channel_id=1, source_target_pairs={{0,3},{1,2},{2,1},{3,0},{4,7},{5,6},{6,5},{7,4},{8,11},{9,10},{10,... | collective-permute-start | bytes 270344 | tf_op jit(solution)/shard_map/ppermute | solution.py:364
  37.8 0.0 collective-permute-done.6.a0
  37.8 1.1 %collective-permute-start.8 = (s32[72,256]{1,0:T(8,128)S(1)}, s32[72,256]{1,0:T(8,128)S(1)}, u32[]{:S(2)}, u32[]{:S(2)}) collective-permute-start(s32[72,256]{1,0:T(8,128)S(1)} %get-tuple-element.30), channel_id=1, source_target_pairs={{0,30},{1,27},{2,28},{3,25},{4,2},{5,31},{6,0},{7,29},{8,6},{9,3},... | collective-permute-start | bytes 221192 | tf_op jit(solution)/shard_map/ppermute | solution.py:364
  39.0 0.0 collective-permute-done.7.a1
  39.0 1.8 %collective-permute-start.9 = (s32[72,256]{1,0:T(8,128)S(1)}, s32[72,256]{1,0:T(8,128)S(1)}, u32[]{:S(2)}, u32[]{:S(2)}) collective-permute-start(s32[72,256]{1,0:T(8,128)S(1)} %get-tuple-element.31), channel_id=1, source_target_pairs={{0,31},{1,26},{2,29},{3,24},{4,3},{5,30},{6,1},{7,28},{8,7},{9,2},... | collective-permute-start | bytes 221192 | tf_op jit(solution)/shard_map/ppermute | solution.py:364
  40.8 9.4 %collective-permute-done.8.a2 = s32[72,256]{1,0:T(8,128)S(1)} collective-permute-done((s32[72,256]{1,0:T(8,128)S(1)}, s32[72,256]{1,0:T(8,128)S(1)}, u32[]{:S(2)}, u32[]{:S(2)}) %collective-permute-start.8) | collective-permute-done | bytes 73760 | tf_op jit(solution)/shard_map/ppermute | solution.py:364
  50.2 0.0 collective-permute-done.9.a3
  50.2 0.0 collective-permute-done.3.b1
  50.2 0.0 collective-permute-done.4.b2
  50.2 0.0 collective-permute-done.5.b3
  50.2 1.9 %shard_map.63 = (f32[32,4,128]{2,1,0:T(4,128)}, f32[1,16]{1,0:T(1,128)}) custom-call(s32[88,256]{1,0:T(8,128)S(1)} %get-tuple-element.24.b0, s32[88,256]{1,0:T(8,128)S(1)} %collective-permute-done.3.b1, s32[88,256]{1,0:T(8,128)S(1)} %collective-permute-done.4.b2, s32[88,256]{1,0:T(8,128)S(1)} %collective-permute-done.5.b3, ...), custom_call_target="tpu_custom_call" | custom-call | tf_op jit(solution)/shard_map/pallas_call | solution.py:323
Async XLA Ops:
  0.6 4.2 %copy-start = (bf16[512,2,128]{2,1,0:T(2,128)(2,1)S(1)}, bf16[512,2,128]{2,1,0:T(2,128)(2,1)}, u32[]{:S(2)}) copy-start(bf16[512,2,128]{2,1,0:T(2,128)(2,1)} %param.4) | copy-start | bytes 786436
  1.7 18.5 %collective-permute-start = (bf16[1032,128]{1,0:T(8,128)(2,1)S(1)}, bf16[1032,128]{1,0:T(8,128)(2,1)S(1)}, u32[]{:S(2)}, u32[]{:S(2)}) collective-permute-start(bf16[1032,128]{1,0:T(8,128)(2,1)S(1)} %get-tuple-element.18.geno.own0), channel_id=1, source_target_pairs={{0,1},{1,0},{2,3},{3,2},{4,5},{5,4},{6,7},{7,6},{8,9},{9,8},{10,11... | collective-permute-start | bytes 792584 | tf_op jit(solution)/shard_map/ppermute | solution.py:364
  4.8 15.4 %collective-permute-start.2 = (bf16[1024,128]{1,0:T(8,128)(2,1)S(1)}, bf16[1024,128]{1,0:T(8,128)(2,1)S(1)}, u32[]{:S(2)}, u32[]{:S(2)}) collective-permute-start(bf16[1024,128]{1,0:T(8,128)(2,1)S(1)} %bitcast.9), channel_id=1, source_target_pairs={{0,9},{1,4},{2,11},{3,6},{4,13},{5,8},{6,15},{7,10},{8,17},{9,12},... | collective-permute-start | bytes 786440 | tf_op jit(solution)/shard_map/ppermute | solution.py:364
  6.2 14.0 %collective-permute-start.1 = (bf16[1024,128]{1,0:T(8,128)(2,1)S(1)}, bf16[1024,128]{1,0:T(8,128)(2,1)S(1)}, u32[]{:S(2)}, u32[]{:S(2)}) collective-permute-start(bf16[1024,128]{1,0:T(8,128)(2,1)S(1)} %bitcast.10), channel_id=1, source_target_pairs={{0,4},{1,9},{2,6},{3,11},{4,8},{5,13},{6,10},{7,15},{8,12},{9,17},... | collective-permute-start | bytes 786440 | tf_op jit(solution)/shard_map/ppermute | solution.py:364
  15.6 16.0 %all-to-all-start = ((bf16[8,8,512]{2,1,0:T(8,128)(2,1)}), bf16[8,8,512]{2,1,0:T(8,128)(2,1)S(1)}, u32[]{:S(2)}, u32[]{:S(2)}) async-start(bf16[8,8,512]{2,1,0:T(8,128)(2,1)} %bitcast.4), calls=%async_computation | async-start | bytes 131072 | tf_op jit(solution)/shard_map/all_to_all | solution.py:387
  21.6 16.3 %collective-permute-start.6 = (s32[72,256]{1,0:T(8,128)S(1)}, s32[72,256]{1,0:T(8,128)S(1)}, u32[]{:S(2)}, u32[]{:S(2)}) collective-permute-start(s32[72,256]{1,0:T(8,128)S(1)} %get-tuple-element.28), channel_id=1, source_target_pairs={{0,28},{1,25},{2,30},{3,27},{4,0},{5,29},{6,2},{7,31},{8,4},{9,1},... | collective-permute-start | bytes 221192 | tf_op jit(solution)/shard_map/ppermute | solution.py:364
  24.3 14.7 %collective-permute-start.7 = (s32[72,256]{1,0:T(8,128)S(1)}, s32[72,256]{1,0:T(8,128)S(1)}, u32[]{:S(2)}, u32[]{:S(2)}) collective-permute-start(s32[72,256]{1,0:T(8,128)S(1)} %get-tuple-element.29), channel_id=1, source_target_pairs={{0,29},{1,24},{2,31},{3,26},{4,1},{5,28},{6,3},{7,30},{8,5},{9,0},... | collective-permute-start | bytes 221192 | tf_op jit(solution)/shard_map/ppermute | solution.py:364
  33.4 16.8 %collective-permute-start.3 = (s32[88,256]{1,0:T(8,128)S(1)}, s32[88,256]{1,0:T(8,128)S(1)}, u32[]{:S(2)}, u32[]{:S(2)}) collective-permute-start(s32[88,256]{1,0:T(8,128)S(1)} %get-tuple-element.25), channel_id=1, source_target_pairs={{0,1},{1,0},{2,3},{3,2},{4,5},{5,4},{6,7},{7,6},{8,9},{9,8},{10,11... | collective-permute-start | bytes 270344 | tf_op jit(solution)/shard_map/ppermute | solution.py:364
  34.7 15.5 %collective-permute-start.4 = (s32[88,256]{1,0:T(8,128)S(1)}, s32[88,256]{1,0:T(8,128)S(1)}, u32[]{:S(2)}, u32[]{:S(2)}) collective-permute-start(s32[88,256]{1,0:T(8,128)S(1)} %get-tuple-element.26), channel_id=1, source_target_pairs={{0,2},{1,3},{2,0},{3,1},{4,6},{5,7},{6,4},{7,5},{8,10},{9,11},{10,... | collective-permute-start | bytes 270344 | tf_op jit(solution)/shard_map/ppermute | solution.py:364
  37.2 13.0 %collective-permute-start.5 = (s32[88,256]{1,0:T(8,128)S(1)}, s32[88,256]{1,0:T(8,128)S(1)}, u32[]{:S(2)}, u32[]{:S(2)}) collective-permute-start(s32[88,256]{1,0:T(8,128)S(1)} %get-tuple-element.27), channel_id=1, source_target_pairs={{0,3},{1,2},{2,1},{3,0},{4,7},{5,6},{6,5},{7,4},{8,11},{9,10},{10,... | collective-permute-start | bytes 270344 | tf_op jit(solution)/shard_map/ppermute | solution.py:364
  37.8 12.4 %collective-permute-start.8 = (s32[72,256]{1,0:T(8,128)S(1)}, s32[72,256]{1,0:T(8,128)S(1)}, u32[]{:S(2)}, u32[]{:S(2)}) collective-permute-start(s32[72,256]{1,0:T(8,128)S(1)} %get-tuple-element.30), channel_id=1, source_target_pairs={{0,30},{1,27},{2,28},{3,25},{4,2},{5,31},{6,0},{7,29},{8,6},{9,3},... | collective-permute-start | bytes 221192 | tf_op jit(solution)/shard_map/ppermute | solution.py:364
  39.0 11.2 %collective-permute-start.9 = (s32[72,256]{1,0:T(8,128)S(1)}, s32[72,256]{1,0:T(8,128)S(1)}, u32[]{:S(2)}, u32[]{:S(2)}) collective-permute-start(s32[72,256]{1,0:T(8,128)S(1)} %get-tuple-element.31), channel_id=1, source_target_pairs={{0,31},{1,26},{2,29},{3,24},{4,3},{5,30},{6,1},{7,28},{8,7},{9,2},... | collective-permute-start | bytes 221192 | tf_op jit(solution)/shard_map/ppermute | solution.py:364

commit v4 on v3

--- a/solution.py
+++ b/solution.py
@@ -125,15 +125,20 @@
             centred = cells[rows] - MIDDLE * (base + column_sums[c:c + 1]) + (MIDDLE * MIDDLE) * counts[c]
             code = quantized(centred, code_step(counts[c]))
             words = lax.shift_left(code, 16) if c == 0 else words | (code & 0xFFFF)
-        outs[d][0:2 * quarter, :] = words
+        for j in range(2):
+            outs[d][j * 2 * quarter:(j + 1) * 2 * quarter, :] = words[:, j * block:(j + 1) * block]
     return first_slab, column_sums, counts
 
 
-def write_tails(outs, start, samples, columns, own, counts):
-    parts = [fixed(v, 2 * samples) for v in (columns[0:2], own[0:2], counts[0], counts[1])]
-    tail = jnp.concatenate(parts + [jnp.zeros((2, columns.shape[1]), jnp.int32)], axis=0)
+def write_tails(outs, samples, block, groups):
+    rows = []
+    for group in groups:
+        for row in group:
+            rows += [row[:, j:j + block] for j in range(0, row.shape[1], block)]
+    rows.append(jnp.zeros((8 - len(rows), block), F32))
+    tail = fixed(jnp.concatenate(rows[:-1] if len(rows) == 9 else rows, axis=0), 2 * samples)
     for out in outs:
-        out[start:start + 8, :] = tail
+        out[block:block + 8, :] = tail
 
 
 def ahead_kernel(own0, own1, other0, other1, label0, a0, a1, a2, a3, sums, wide, left, right):
@@ -141,7 +146,8 @@
     classes = class_rows(label0, own1[2 * samples:, :])
     outs = (a0, a1, a2, a3)
     _, columns, counts = coded_tiles((other0, other1), (own0, own1), classes, left, right, wide, outs)
-    write_tails(outs, wide.shape[1] // 2, samples, columns, columns, counts)
+    block = wide.shape[1]
+    write_tails(outs, samples, block, ((columns[0:1], columns[1:2]), (counts[0][:, 0:block], counts[1][:, 0:block])))
     sums[...] = columns
 
 
@@ -152,7 +158,7 @@
     classes = class_rows(label0, own1[2 * samples:, :])
     outs = (b0, b1, b2, b3)
     own_slab, columns, counts = coded_tiles((own0, own1), (other0, other1), classes, left, right, wide, outs)
-    write_tails(outs, block // 2, samples, columns, sums[...], counts)
+    write_tails(outs, samples, block, ((columns[0:1], columns[1:2]), (sums[0:1, :], sums[1:2, :])))
 
     pairs = peer_ids.shape[1]
     rows = got.shape[0]
@@ -181,13 +187,14 @@
         for c in range(2):
             for i in range(2):
                 values.append(jnp.sum(side[i] * slab[c], axis=1, keepdims=True))
-    lane = iota((pairs, 2 * block), 1)
-    refit = jnp.zeros((pairs, 2 * block), F32)
+    values += [jnp.broadcast_to(counts[c][:, 0:1], (pairs, 1)) for c in range(2)]
+    lane = iota((pairs, block), 1)
+    refit = jnp.zeros((pairs, block), F32)
     for v, value in enumerate(values):
         refit = jnp.where(lane == v, value, refit)
     refit = fixed(refit, 2 * samples)
     for out in outs:
-        out[block // 2 + 8:, :] = refit
+        out[block + 8:, :] = refit
 
 
 def complete(cells, margin_a, margin_b, totals):
@@ -233,17 +240,20 @@
 def finish_kernel(b0, b1, b2, b3, a0, a1, a2, a3, screen, stat, columns, *, samples):
     k = lax.axis_index("samp")
     bs, as_ = (b0, b1, b2, b3), (a0, a1, a2, a3)
-    block = b0.shape[1] // 2
+    block = b0.shape[1]
     quarter = block // 4
-    height = 2 * quarter
     pairs = stat.shape[1]
 
-    def both(x, y, row, lanes=slice(0, block)):
-        return floating(x[row:row + 1, lanes], 2 * samples) + floating(y[row:row + 1, lanes], 2 * samples)
-
-    lanes_of = [slice(j * block, (j + 1) * block) for j in range(2)]
-    totals_row = [both(b0, b2, height + 4 + c) for c in range(2)]
-    own = [both(b0, b2, height + 2 + c, lanes_of[i]) for c in range(2) for i in range(2)]
+    def value(m, row):
+        return floating(m[row:row + 1, :], 2 * samples)
+
+    def count(m, c):
+        if m.shape[0] == block + 8:
+            return value(m, block + 4 + c)
+        return jnp.broadcast_to(floating(m[block + 8:block + 9, 16 + c:17 + c], 2 * samples), (1, block))
+
+    totals_row = [count(b0, c) + count(b2, c) for c in range(2)]
+    own = [value(b0, block + 4 + v) + value(b2, block + 4 + v) for v in range(4)]
     columns[...] = jnp.concatenate(own + [jnp.zeros((block - 4, block), F32)], axis=0).T
     mine = columns[pl.ds(pl.multiple_of(k * quarter, quarter), quarter), :]
     margin_a = [[jnp.broadcast_to(mine[:, c * 2 + i:c * 2 + i + 1], (quarter, block)) for i in range(2)] for c in range(2)]
@@ -252,13 +262,13 @@
     for msgs in (bs, as_):
         for parity in range(2):
             x, y = msgs[parity], msgs[parity + 2]
-            steps = [[code_step(floating(m[height + 4 + c:height + 5 + c, 0:block], 2 * samples)) for m in (x, y)]
-                     for c in range(2)]
-            margin_b = [[both(x, y, height + c, lanes_of[j]) for j in range(2)] for c in range(2)]
+            steps = [[code_step(count(m, c)) for m in (x, y)] for c in range(2)]
+            margin_b = [[value(x, block + c * 2 + j) + value(y, block + c * 2 + j) for j in range(2)] for c in range(2)]
             cells = [[[None, None], [None, None]] for _ in range(2)]
             for i in range(2):
                 for j in range(2):
-                    words = [m[i * quarter:(i + 1) * quarter, lanes_of[j]] for m in (x, y)]
+                    start = (j * 2 + i) * quarter
+                    words = [m[start:start + quarter, :] for m in (x, y)]
                     for c in range(2):
                         codes = [lax.shift_right_arithmetic(w if c == 0 else lax.shift_left(w, 16), 16) for w in words]
                         base = MIDDLE * (margin_a[c][i] + margin_b[c][j]) - (MIDDLE * MIDDLE) * totals_row[c]
@@ -272,11 +282,11 @@
         screen[:, 2 * side + 1, :] = jnp.where(even, o, e)
 
     for start in range(0, pairs, block):
-        count = min(block, pairs - start)
-        rows = slice(height + 8 + start, height + 8 + start + count)
+        take = min(block, pairs - start)
+        rows = slice(block + 8 + start, block + 8 + start + take)
         sums = floating(b0[rows, 0:block] + b1[rows, 0:block] + b2[rows, 0:block] + b3[rows, 0:block], 2 * samples)
-        if count < block:
-            sums = jnp.concatenate([sums, jnp.ones((block - count, block), F32)], axis=0)
+        if take < block:
+            sums = jnp.concatenate([sums, jnp.ones((block - take, block), F32)], axis=0)
         turned = sums.T
         row = [turned[v:v + 1, :] for v in range(16)]
         cells = [[[row[c * 4 + i * 2 + j] for j in range(2)] for i in range(2)] for c in range(2)]
@@ -312,7 +322,7 @@
                 for j in range(3):
                     term = n[c][i][j] * jnp.log(n[c][i][j] / fitted[c * 9 + i * 3 + j])
                     total = term if total is None else total + term
-        stat[:, start:start + count] = (2.0 * total)[:, 0:count]
+        stat[:, start:start + take] = (2.0 * total)[:, 0:take]
 
 
 def vmem(count):
@@ -367,14 +377,15 @@
     labels = case_labels.reshape(1, samples)
     row_of = lambda count: pltpu.VMEM((1, count), jnp.int32)
     height = 2 * samples + samples // block + -(samples // block) % 8
-    marked, labels, own_ids, peer_ids, placed = pl.pallas_call(
+    stage = pl.pallas_call(
         stage_kernel,
         out_shape=[pltpu.VMEM((height, block), BF16), row_of(samples), row_of(pairs), row_of(pairs),
                    pltpu.VMEM((snp_count, pairs), jnp.int32)],
         in_specs=[pl.BlockSpec(memory_space=pl.ANY)] * 4,
         out_specs=vmem(5),
         scratch_shapes=[pltpu.SemaphoreType.DMA((4,))],
-    )(geno, labels, refit_own[None, :], refit_peer[None, :])
+    )
+    marked, labels, own_ids, peer_ids, placed = stage(geno, labels, refit_own[None, :], refit_peer[None, :])
     other0 = moved(geno, lambda b, k: (b + 1 + (k & 1), k))
     other1 = moved(geno, lambda b, k: (b + 2 - (k & 1), k ^ 1))
     own1 = moved(marked, lambda b, k: (b, k ^ 1))
@@ -386,8 +397,8 @@
     )
     got = lax.all_to_all(sent, "snp", split_axis=0, concat_axis=0, tiled=True)
     scratch = [wide, pltpu.VMEM((4, 4, block // 4, 2 * samples), BF16), pltpu.VMEM((2 * samples, 2 * block), BF16)]
-    short = jax.ShapeDtypeStruct((block // 2 + 8, 2 * block), jnp.int32)
-    tall = jax.ShapeDtypeStruct((block // 2 + 8 + pairs, 2 * block), jnp.int32)
+    short = jax.ShapeDtypeStruct((block + 8, block), jnp.int32)
+    tall = jax.ShapeDtypeStruct((block + 8 + pairs, block), jnp.int32)
     *ahead, sums = run(
         ahead_kernel, (marked, own1, other0, other1, labels),
         [short] * 4 + [jax.ShapeDtypeStruct((8, 2 * block), F32)], scratch,

time: 52.7 us -> 58.7 us (1.11)
  waiting for transfers between devices: 9.42 us -> 19.7 us
  starting transfers between devices: 26.5 us -> 16.7 us
  blocking collectives: 8.27 us -> 14.6 us
  Pallas kernels: 7.24 us -> 6.56 us
    ppermute x10, waiting for transfers between devices: 9.41 us -> 19.7 us  [moved(): return lax.ppermute(value, ('snp', 'samp'), links)]
    all_to_all x0 -> x1, blocking collectives: none -> 8.22 us  [on_device(): got = lax.all_to_all(sent, 'snp', split_axis=0, concat_axis=0, tiled=True)]
    ppermute x10, starting transfers between devices: 22 us -> 16.7 us  [moved(): return lax.ppermute(value, ('snp', 'samp'), links)]
    all_to_all x1 -> x0, starting transfers between devices: 4.57 us -> none  [on_device(): got = lax.all_to_all(sent, 'snp', split_axis=0, concat_axis=0, tiled=True)]
    psum x1, blocking collectives: 8.27 us -> 6.36 us  [on_device(): ids = lax.psum(placed, 'snp')]
    pallas_call x4, Pallas kernels: 6.19 us -> 5.51 us  [run(): pl.pallas_call(body, out_shape=[pltpu.VMEM(o.shape, o.dtype) if near else...]
  transfers between devices with their start and end apart: 11 -> 10, of which waited for: 1 -> 2; matrix products, arithmetic and copies ran while one was open for 0% -> 0% of each run, Pallas kernels for 8% -> 4%
where the time goes in v4:
time: 58.7 us; the launch traced here: 58.2 us
  waiting for transfers between devices  19.7 us (34%)
  starting transfers between devices  16.7 us (28%)
  blocking collectives  14.6 us (25%)
  Pallas kernels  6.56 us (11%)
  between operations  0.69 us (1%)
    ppermute x10, waiting for transfers between devices, moved(): return lax.ppermute(value, ('snp', 'samp'), links)  19.7 us
    ppermute x10, starting transfers between devices, moved(): return lax.ppermute(value, ('snp', 'samp'), links)  16.7 us
    all_to_all x1, blocking collectives, on_device(): got = lax.all_to_all(sent, 'snp', split_axis=0, concat_axis=0, tiled=True)  8.22 us
    psum x1, blocking collectives, on_device(): ids = lax.psum(placed, 'snp')  6.36 us
    pallas_call x4, Pallas kernels, run(): pl.pallas_call(body, out_shape=[pltpu.VMEM(o.shape, o.dtype) if near else...  5.51 us
  transfers between devices with their start and end apart: 10, of which 2 were waited for; matrix products, arithmetic and copies ran while one was open for 0% of the time, Pallas kernels for 4%

profile of v4, /device:TPU:0, one launch (start us, length us, event | category | flops | bytes accessed | tf_op | source)
XLA Modules:
  0.0 58.2 jit_solution(11464785117068110521)
XLA Ops:
  0.6 0.0 copy-start
  0.6 1.1 %shard_map.59 = (bf16[1032,128]{1,0:T(8,128)(2,1)S(1)}, s32[1,512]{1,0:T(1,128)S(1)}, s32[1,16]{1,0:T(1,128)S(1)}, s32[1,16]{1,0:T(1,128)S(1)}, s32[8,16]{1,0:T(8,128)S(1)}) custom-call(bf16[1024,128]{1,0:T(8,128)(2,1)} %bitcast.9, s32[1,512]{1,0:T(1,128)} %bitcast.12, s32[1,16]{1,0:T(1,128)} %bitcast.13, s32[1,16]{1,0:T(1,128)} %bitcast.14), custom_call_target="tpu_custom_call" | custom-call | tf_op jit(solution)/shard_map/pallas_call | solution.py:388
  1.7 3.1 %collective-permute-start = (bf16[1032,128]{1,0:T(8,128)(2,1)S(1)}, bf16[1032,128]{1,0:T(8,128)(2,1)S(1)}, u32[]{:S(2)}, u32[]{:S(2)}) collective-permute-start(bf16[1032,128]{1,0:T(8,128)(2,1)S(1)} %get-tuple-element.18.geno.own0), channel_id=1, source_target_pairs={{0,1},{1,0},{2,3},{3,2},{4,5},{5,4},{6,7},{7,6},{8,9},{9,8},{10,11... | collective-permute-start | bytes 792584 | tf_op jit(solution)/shard_map/ppermute | solution.py:374
  4.8 0.0 copy-done
  4.8 1.4 %collective-permute-start.2 = (bf16[1024,128]{1,0:T(8,128)(2,1)S(1)}, bf16[1024,128]{1,0:T(8,128)(2,1)S(1)}, u32[]{:S(2)}, u32[]{:S(2)}) collective-permute-start(bf16[1024,128]{1,0:T(8,128)(2,1)S(1)} %bitcast.10), channel_id=1, source_target_pairs={{0,9},{1,4},{2,11},{3,6},{4,13},{5,8},{6,15},{7,10},{8,17},{9,12},... | collective-permute-start | bytes 786440 | tf_op jit(solution)/shard_map/ppermute | solution.py:374
  6.2 0.0 collective-permute-start.1
  6.2 11.5 %collective-permute-done.2.other1 = bf16[1024,128]{1,0:T(8,128)(2,1)S(1)} collective-permute-done((bf16[1024,128]{1,0:T(8,128)(2,1)S(1)}, bf16[1024,128]{1,0:T(8,128)(2,1)S(1)}, u32[]{:S(2)}, u32[]{:S(2)}) %collective-permute-start.2) | collective-permute-done | bytes 262176 | tf_op jit(solution)/shard_map/ppermute | solution.py:374
  17.7 0.0 collective-permute-done.1.other0
  17.7 0.0 collective-permute-done.own1
  17.7 1.4 %shard_map.61 = (s32[136,128]{1,0:T(8,128)S(1)}, s32[136,128]{1,0:T(8,128)S(1)}, s32[136,128]{1,0:T(8,128)S(1)}, s32[136,128]{1,0:T(8,128)S(1)}, f32[8,256]{1,0:T(8,128)S(1)}) custom-call(bf16[1032,128]{1,0:T(8,128)(2,1)S(1)} %get-tuple-element.18.geno.own0, bf16[1032,128]{1,0:T(8,128)(2,1)S(1)} %collective-permute-done.own1, ...), custom_call_target="tpu_custom_call" | custom-call | tf_op jit(solution)/shard_map/pallas_call | solution.py:333
  19.1 1.2 %collective-permute-start.6 = (s32[136,128]{1,0:T(8,128)S(1)}, s32[136,128]{1,0:T(8,128)S(1)}, u32[]{:S(2)}, u32[]{:S(2)}) collective-permute-start(s32[136,128]{1,0:T(8,128)S(1)} %get-tuple-element.28), channel_id=1, source_target_pairs={{0,28},{1,25},{2,30},{3,27},{4,0},{5,29},{6,2},{7,31},{8,4},{9,1},... | collective-permute-start | bytes 208904 | tf_op jit(solution)/shard_map/ppermute | solution.py:374
  20.3 4.4 %collective-permute-start.7 = (s32[136,128]{1,0:T(8,128)S(1)}, s32[136,128]{1,0:T(8,128)S(1)}, u32[]{:S(2)}, u32[]{:S(2)}) collective-permute-start(s32[136,128]{1,0:T(8,128)S(1)} %get-tuple-element.29), channel_id=1, source_target_pairs={{0,29},{1,24},{2,31},{3,26},{4,1},{5,28},{6,3},{7,30},{8,5},{9,0},... | collective-permute-start | bytes 208904 | tf_op jit(solution)/shard_map/ppermute | solution.py:374
  24.7 6.4 %psum.7.ids = s32[8,16]{1,0:T(8,128)S(1)} all-reduce(s32[8,16]{1,0:T(8,128)S(1)} %get-tuple-element.22), channel_id=1, replica_groups=mesh['snp'=8,'samp'=4] {'snp'}, use_global_device_ids=true, to_apply=%region_0.0 | all-reduce | flops 128 | bytes 1024 | tf_op jit(solution)/shard_map/psum | solution.py:392
  31.1 0.5 shard_map.60
  31.6 8.2 %all_to_all.11 = bf16[8,8,512]{2,1,0:T(8,128)(2,1)S(1)} all-to-all(bf16[8,8,512]{2,1,0:T(8,128)(2,1)S(1)} %bitcast.8), channel_id=1, replica_groups=mesh['snp'=8,'samp'=4] {'snp'}, dimensions={0} | all-to-all | bytes 131072 | tf_op jit(solution)/shard_map/all_to_all | solution.py:398
  39.8 1.8 %shard_map.62 = (s32[152,128]{1,0:T(8,128)S(1)}, s32[152,128]{1,0:T(8,128)S(1)}, s32[152,128]{1,0:T(8,128)S(1)}, s32[152,128]{1,0:T(8,128)S(1)}) custom-call(bf16[1032,128]{1,0:T(8,128)(2,1)S(1)} %get-tuple-element.18.geno.own0, bf16[1032,128]{1,0:T(8,128)(2,1)S(1)} %collective-permute-done.own1, bf16[1024,128]{1,0:T(8,128)(2,1)S(1)} %collective-permute-done.1.other0, ...), custom_call_target="tpu_custom_call" | custom-call | tf_op jit(solution)/shard_map/pallas_call | solution.py:333
  41.6 0.4 collective-permute-start.3
  41.9 2.6 %collective-permute-start.4 = (s32[152,128]{1,0:T(8,128)S(1)}, s32[152,128]{1,0:T(8,128)S(1)}, u32[]{:S(2)}, u32[]{:S(2)}) collective-permute-start(s32[152,128]{1,0:T(8,128)S(1)} %get-tuple-element.26), channel_id=1, source_target_pairs={{0,2},{1,3},{2,0},{3,1},{4,6},{5,7},{6,4},{7,5},{8,10},{9,11},{10,... | collective-permute-start | bytes 233480 | tf_op jit(solution)/shard_map/ppermute | solution.py:374
  44.5 1.5 %collective-permute-start.5 = (s32[152,128]{1,0:T(8,128)S(1)}, s32[152,128]{1,0:T(8,128)S(1)}, u32[]{:S(2)}, u32[]{:S(2)}) collective-permute-start(s32[152,128]{1,0:T(8,128)S(1)} %get-tuple-element.27), channel_id=1, source_target_pairs={{0,3},{1,2},{2,1},{3,0},{4,7},{5,6},{6,5},{7,4},{8,11},{9,10},{10,... | collective-permute-start | bytes 233480 | tf_op jit(solution)/shard_map/ppermute | solution.py:374
  46.0 0.0 collective-permute-done.6.a0
  46.0 0.4 collective-permute-start.8
  46.4 0.0 collective-permute-done.7.a1
  46.4 1.7 %collective-permute-start.9 = (s32[136,128]{1,0:T(8,128)S(1)}, s32[136,128]{1,0:T(8,128)S(1)}, u32[]{:S(2)}, u32[]{:S(2)}) collective-permute-start(s32[136,128]{1,0:T(8,128)S(1)} %get-tuple-element.31), channel_id=1, source_target_pairs={{0,31},{1,26},{2,29},{3,24},{4,3},{5,30},{6,1},{7,28},{8,7},{9,2},... | collective-permute-start | bytes 208904 | tf_op jit(solution)/shard_map/ppermute | solution.py:374
  48.1 8.2 %collective-permute-done.8.a2 = s32[136,128]{1,0:T(8,128)S(1)} collective-permute-done((s32[136,128]{1,0:T(8,128)S(1)}, s32[136,128]{1,0:T(8,128)S(1)}, u32[]{:S(2)}, u32[]{:S(2)}) %collective-permute-start.8) | collective-permute-done | bytes 69664 | tf_op jit(solution)/shard_map/ppermute | solution.py:374
  56.3 0.0 collective-permute-done.9.a3
  56.3 0.0 collective-permute-done.3.b1
  56.3 0.0 collective-permute-done.4.b2
  56.3 0.0 collective-permute-done.5.b3
  56.3 1.9 %shard_map.63 = (f32[32,4,128]{2,1,0:T(4,128)}, f32[1,16]{1,0:T(1,128)}) custom-call(s32[152,128]{1,0:T(8,128)S(1)} %get-tuple-element.24.b0, s32[152,128]{1,0:T(8,128)S(1)} %collective-permute-done.3.b1, s32[152,128]{1,0:T(8,128)S(1)} %collective-permute-done.4.b2, s32[152,128]{1,0:T(8,128)S(1)} %collective-permute-done.5.b3, ...), custom_call_target="tpu_custom_call" | custom-call | tf_op jit(solution)/shard_map/pallas_call | solution.py:333
Async XLA Ops:
  0.6 4.2 %copy-start = (bf16[512,2,128]{2,1,0:T(2,128)(2,1)S(1)}, bf16[512,2,128]{2,1,0:T(2,128)(2,1)}, u32[]{:S(2)}) copy-start(bf16[512,2,128]{2,1,0:T(2,128)(2,1)} %param.4) | copy-start | bytes 786436
  1.7 16.0 %collective-permute-start = (bf16[1032,128]{1,0:T(8,128)(2,1)S(1)}, bf16[1032,128]{1,0:T(8,128)(2,1)S(1)}, u32[]{:S(2)}, u32[]{:S(2)}) collective-permute-start(bf16[1032,128]{1,0:T(8,128)(2,1)S(1)} %get-tuple-element.18.geno.own0), channel_id=1, source_target_pairs={{0,1},{1,0},{2,3},{3,2},{4,5},{5,4},{6,7},{7,6},{8,9},{9,8},{10,11... | collective-permute-start | bytes 792584 | tf_op jit(solution)/shard_map/ppermute | solution.py:374
  4.8 12.9 %collective-permute-start.2 = (bf16[1024,128]{1,0:T(8,128)(2,1)S(1)}, bf16[1024,128]{1,0:T(8,128)(2,1)S(1)}, u32[]{:S(2)}, u32[]{:S(2)}) collective-permute-start(bf16[1024,128]{1,0:T(8,128)(2,1)S(1)} %bitcast.10), channel_id=1, source_target_pairs={{0,9},{1,4},{2,11},{3,6},{4,13},{5,8},{6,15},{7,10},{8,17},{9,12},... | collective-permute-start | bytes 786440 | tf_op jit(solution)/shard_map/ppermute | solution.py:374
  6.2 11.5 %collective-permute-start.1 = (bf16[1024,128]{1,0:T(8,128)(2,1)S(1)}, bf16[1024,128]{1,0:T(8,128)(2,1)S(1)}, u32[]{:S(2)}, u32[]{:S(2)}) collective-permute-start(bf16[1024,128]{1,0:T(8,128)(2,1)S(1)} %bitcast.11), channel_id=1, source_target_pairs={{0,4},{1,9},{2,6},{3,11},{4,8},{5,13},{6,10},{7,15},{8,12},{9,17},... | collective-permute-start | bytes 786440 | tf_op jit(solution)/shard_map/ppermute | solution.py:374
  19.1 26.9 %collective-permute-start.6 = (s32[136,128]{1,0:T(8,128)S(1)}, s32[136,128]{1,0:T(8,128)S(1)}, u32[]{:S(2)}, u32[]{:S(2)}) collective-permute-start(s32[136,128]{1,0:T(8,128)S(1)} %get-tuple-element.28), channel_id=1, source_target_pairs={{0,28},{1,25},{2,30},{3,27},{4,0},{5,29},{6,2},{7,31},{8,4},{9,1},... | collective-permute-start | bytes 208904 | tf_op jit(solution)/shard_map/ppermute | solution.py:374
  20.3 26.2 %collective-permute-start.7 = (s32[136,128]{1,0:T(8,128)S(1)}, s32[136,128]{1,0:T(8,128)S(1)}, u32[]{:S(2)}, u32[]{:S(2)}) collective-permute-start(s32[136,128]{1,0:T(8,128)S(1)} %get-tuple-element.29), channel_id=1, source_target_pairs={{0,29},{1,24},{2,31},{3,26},{4,1},{5,28},{6,3},{7,30},{8,5},{9,0},... | collective-permute-start | bytes 208904 | tf_op jit(solution)/shard_map/ppermute | solution.py:374
  41.6 14.7 %collective-permute-start.3 = (s32[152,128]{1,0:T(8,128)S(1)}, s32[152,128]{1,0:T(8,128)S(1)}, u32[]{:S(2)}, u32[]{:S(2)}) collective-permute-start(s32[152,128]{1,0:T(8,128)S(1)} %get-tuple-element.25), channel_id=1, source_target_pairs={{0,1},{1,0},{2,3},{3,2},{4,5},{5,4},{6,7},{7,6},{8,9},{9,8},{10,11... | collective-permute-start | bytes 233480 | tf_op jit(solution)/shard_map/ppermute | solution.py:374
  41.9 14.4 %collective-permute-start.4 = (s32[152,128]{1,0:T(8,128)S(1)}, s32[152,128]{1,0:T(8,128)S(1)}, u32[]{:S(2)}, u32[]{:S(2)}) collective-permute-start(s32[152,128]{1,0:T(8,128)S(1)} %get-tuple-element.26), channel_id=1, source_target_pairs={{0,2},{1,3},{2,0},{3,1},{4,6},{5,7},{6,4},{7,5},{8,10},{9,11},{10,... | collective-permute-start | bytes 233480 | tf_op jit(solution)/shard_map/ppermute | solution.py:374
  44.5 11.8 %collective-permute-start.5 = (s32[152,128]{1,0:T(8,128)S(1)}, s32[152,128]{1,0:T(8,128)S(1)}, u32[]{:S(2)}, u32[]{:S(2)}) collective-permute-start(s32[152,128]{1,0:T(8,128)S(1)} %get-tuple-element.27), channel_id=1, source_target_pairs={{0,3},{1,2},{2,1},{3,0},{4,7},{5,6},{6,5},{7,4},{8,11},{9,10},{10,... | collective-permute-start | bytes 233480 | tf_op jit(solution)/shard_map/ppermute | solution.py:374
  46.0 10.3 %collective-permute-start.8 = (s32[136,128]{1,0:T(8,128)S(1)}, s32[136,128]{1,0:T(8,128)S(1)}, u32[]{:S(2)}, u32[]{:S(2)}) collective-permute-start(s32[136,128]{1,0:T(8,128)S(1)} %get-tuple-element.30), channel_id=1, source_target_pairs={{0,30},{1,27},{2,28},{3,25},{4,2},{5,31},{6,0},{7,29},{8,6},{9,3},... | collective-permute-start | bytes 208904 | tf_op jit(solution)/shard_map/ppermute | solution.py:374
  46.4 9.9 %collective-permute-start.9 = (s32[136,128]{1,0:T(8,128)S(1)}, s32[136,128]{1,0:T(8,128)S(1)}, u32[]{:S(2)}, u32[]{:S(2)}) collective-permute-start(s32[136,128]{1,0:T(8,128)S(1)} %get-tuple-element.31), channel_id=1, source_target_pairs={{0,31},{1,26},{2,29},{3,24},{4,3},{5,30},{6,1},{7,28},{8,7},{9,2},... | collective-permute-start | bytes 208904 | tf_op jit(solution)/shard_map/ppermute | solution.py:374

commit v5 on v4

--- a/solution.py
+++ b/solution.py
@@ -11,6 +11,7 @@
 CAP = 4
 ITERS = 10
 MIDDLE = 0.47
+GRANT = 24 << 20
 SPREAD = 0.411
 F32 = jnp.float32
 BF16 = jnp.bfloat16
@@ -88,32 +89,44 @@
     return [case, 1.0 - case]
 
 
-def coded_tiles(first_refs, second_refs, classes, left, right, wide, outs):
+def turn(parts, classes, half, left):
     k = lax.axis_index("samp")
-    samples = wide.shape[0] // 2
-    block = wide.shape[1]
+    samples, block = parts[0].shape
     quarter = block // 4
-    first_slab = None
-    for half in range(2):
-        rows = pl.ds(half * samples, samples)
-        parts = split_genotypes(first_refs[half], wide)
-        if half == 0:
-            first_slab = [p.astype(BF16) for p in parts]
-        for i in range(2):
-            turned = parts[i].T
-            for c in range(2):
-                piece = (turned * classes[c][:, half * samples:(half + 1) * samples]).astype(BF16)
-                for q in range(4):
-                    d = q ^ k
-                    left[d, c * 2 + i, :, rows] = piece[q * quarter:(q + 1) * quarter]
-        parts = split_genotypes(second_refs[half], wide)
-        for j in range(2):
-            right[rows, j * block:(j + 1) * block] = parts[j].astype(BF16)
-    lhs = left[...].reshape(16 * quarter, 2 * samples)
-    cells = dot(lhs, right[...])
-    row_sums = dot(lhs, jnp.ones((2 * samples, block), BF16))
+    for i in range(2):
+        turned = parts[i].T
+        for c in range(2):
+            piece = (turned * classes[c][:, half * samples:(half + 1) * samples]).astype(BF16)
+            for q in range(4):
+                left[q ^ k, c * 2 + i] = piece[q * quarter:(q + 1) * quarter]
+
+
+def lay(parts, right):
+    block = parts[0].shape[1]
+    for j in range(2):
+        right[:, j * block:(j + 1) * block] = parts[j].astype(BF16)
+
+
+def prepare_kernel(own0, own1, other1, label0,
+                   own_left0, own_left1, own_right0, own_right1, other_left1, other_right1, wide):
+    classes = class_rows(label0, own1[wide.shape[0]:, :])
+    for ref, half, left, right in ((own0, 0, own_left0, own_right0), (own1, 1, own_left1, own_right1),
+                                   (other1, 1, other_left1, other_right1)):
+        parts = split_genotypes(ref, wide)
+        turn(parts, classes, half, left)
+        lay(parts, right)
+
+
+def coded_tiles(lefts, rights, classes, outs):
+    samples = rights[0].shape[0]
+    block = rights[0].shape[1] // 2
+    quarter = block // 4
+    lhs = [left[...].reshape(16 * quarter, samples) for left in lefts]
+    cells = dot(lhs[0], rights[0][...]) + dot(lhs[1], rights[1][...])
+    ones = jnp.ones((samples, block), BF16)
+    row_sums = dot(lhs[0], ones) + dot(lhs[1], ones)
     weights = jnp.concatenate(classes + [jnp.zeros((6, 2 * samples), F32)], axis=0).astype(BF16)
-    column_sums = dot(weights, right[...])
+    column_sums = dot(weights[:, 0:samples], rights[0][...]) + dot(weights[:, samples:], rights[1][...])
     lanes = jnp.ones((1, 2 * block), F32)
     counts = [jnp.sum(classes[c], axis=1, keepdims=True) * lanes for c in range(2)]
     for d in range(4):
@@ -127,7 +140,7 @@
             words = lax.shift_left(code, 16) if c == 0 else words | (code & 0xFFFF)
         for j in range(2):
             outs[d][j * 2 * quarter:(j + 1) * 2 * quarter, :] = words[:, j * block:(j + 1) * block]
-    return first_slab, column_sums, counts
+    return column_sums, counts
 
 
 def write_tails(outs, samples, block, groups):
@@ -141,23 +154,28 @@
         out[block:block + 8, :] = tail
 
 
-def ahead_kernel(own0, own1, other0, other1, label0, a0, a1, a2, a3, sums, wide, left, right):
-    samples = wide.shape[0] // 2
-    classes = class_rows(label0, own1[2 * samples:, :])
-    outs = (a0, a1, a2, a3)
-    _, columns, counts = coded_tiles((other0, other1), (own0, own1), classes, left, right, wide, outs)
-    block = wide.shape[1]
-    write_tails(outs, samples, block, ((columns[0:1], columns[1:2]), (counts[0][:, 0:block], counts[1][:, 0:block])))
-    sums[...] = columns
-
-
-def behind_kernel(own0, own1, other0, other1, label0, own_ids, peer_ids, got, sums,
-                  b0, b1, b2, b3, wide, left, right, *, shift):
+def ahead_kernel(other0, own1, own_right0, own_right1, other_left1, label0,
+                 a0, a1, a2, a3, sums, other_right0, wide, other_left0):
     samples = wide.shape[0] // 2
     block = wide.shape[1]
     classes = class_rows(label0, own1[2 * samples:, :])
+    outs = (a0, a1, a2, a3)
+    parts = split_genotypes(other0, wide)
+    turn(parts, classes, 0, other_left0)
+    lay(parts, other_right0)
+    columns, counts = coded_tiles((other_left0, other_left1), (own_right0, own_right1), classes, outs)
+    write_tails(outs, samples, block, ((columns[0:1], columns[1:2]), (counts[0][:, 0:block], counts[1][:, 0:block])))
+    sums[...] = columns
+
+
+def behind_kernel(own1, own_left0, own_left1, own_right0, other_right0, other_right1, label0, own_ids, peer_ids, got, sums,
+                  b0, b1, b2, b3, *, shift):
+    samples = own_right0.shape[0]
+    block = own_right0.shape[1] // 2
+    classes = class_rows(label0, own1[2 * samples:, :])
     outs = (b0, b1, b2, b3)
-    own_slab, columns, counts = coded_tiles((own0, own1), (other0, other1), classes, left, right, wide, outs)
+    columns, counts = coded_tiles((own_left0, own_left1), (other_right0, other_right1), classes, outs)
+    own_slab = [own_right0[:, j * block:(j + 1) * block] for j in range(2)]
     write_tails(outs, samples, block, ((columns[0:1], columns[1:2]), (sums[0:1, :], sums[1:2, :])))
 
     pairs = peer_ids.shape[1]
@@ -211,28 +229,35 @@
     return table
 
 
-def kirkwood(n, margin_a, margin_b, totals):
+def row_terms(margin_a, totals):
     row_ic = [[margin_a[c][0], margin_a[c][1], totals[c] - margin_a[c][0] - margin_a[c][1]] for c in range(2)]
+    single = [row_ic[0][i] + row_ic[1][i] for i in range(3)]
+    share = [[row_ic[c][i] / (single[i] * totals[c]) for i in range(3)] for c in range(2)]
+    inverse = [[single[i] * totals[c] / row_ic[c][i] for i in range(3)] for c in range(2)]
+    return share, inverse
+
+
+def kirkwood(n, rows, margin_b, totals):
+    share, inverse = rows
     col_jc = [[margin_b[c][0], margin_b[c][1], totals[c] - margin_b[c][0] - margin_b[c][1]] for c in range(2)]
-    single_a = [row_ic[0][i] + row_ic[1][i] for i in range(3)]
     single_b = [col_jc[0][j] + col_jc[1][j] for j in range(3)]
+    col_y = [[col_jc[c][j] / single_b[j] for j in range(3)] for c in range(2)]
+    col_z = [[single_b[j] / col_jc[c][j] for j in range(3)] for c in range(2)]
     grand = totals[0] + totals[1]
-    inv_a = [1.0 / s for s in single_a]
-    row_x = [[row_ic[c][i] * inv_a[i] / totals[c] for i in range(3)] for c in range(2)]
-    col_y = [[col_jc[c][j] / single_b[j] for j in range(3)] for c in range(2)]
     scale = None
-    approx = {}
+    ratio = {}
     for i in range(3):
         for j in range(3):
             pair = n[0][i][j] + n[1][i][j]
+            inv_pair = 1.0 / pair
             for c in range(2):
-                value = pair * row_x[c][i] * col_y[c][j]
-                approx[c, i, j] = value
+                value = pair * share[c][i] * col_y[c][j]
+                ratio[c, i, j] = n[c][i][j] * (inv_pair * inverse[c][i] * col_z[c][j])
                 scale = value if scale is None else scale + value
     factor = scale / grand
     total = None
-    for (c, i, j), value in approx.items():
-        term = n[c][i][j] * jnp.log(n[c][i][j] * factor / value)
+    for (c, i, j), value in ratio.items():
+        term = n[c][i][j] * jnp.log(value * factor)
         total = term if total is None else total + term
     return 2.0 * total
 
@@ -258,6 +283,7 @@
     mine = columns[pl.ds(pl.multiple_of(k * quarter, quarter), quarter), :]
     margin_a = [[jnp.broadcast_to(mine[:, c * 2 + i:c * 2 + i + 1], (quarter, block)) for i in range(2)] for c in range(2)]
 
+    rows_of = row_terms(margin_a, totals_row)
     stats = []
     for msgs in (bs, as_):
         for parity in range(2):
@@ -274,7 +300,7 @@
                         base = MIDDLE * (margin_a[c][i] + margin_b[c][j]) - (MIDDLE * MIDDLE) * totals_row[c]
                         cells[c][i][j] = (codes[0].astype(F32) * steps[c][0] + codes[1].astype(F32) * steps[c][1]) + base
             table = complete(cells, margin_a, margin_b, totals_row)
-            stats.append(kirkwood(table, margin_a, margin_b, totals_row))
+            stats.append(kirkwood(table, rows_of, margin_b, totals_row))
     even = (k & 1) == 0
     for side in range(2):
         e, o = stats[2 * side], stats[2 * side + 1]
@@ -336,6 +362,7 @@
         in_specs=vmem(len(args)),
         out_specs=vmem(len(outs)),
         scratch_shapes=scratch,
+        compiler_params=pltpu.CompilerParams(vmem_limit_bytes=GRANT),
     )(*(pltpu.with_memory_space_constraint(a, pltpu.VMEM) for a in args))
 
 
@@ -396,19 +423,22 @@
         [jax.ShapeDtypeStruct((snp_count * 2 * CAP, samples), BF16)], [wide],
     )
     got = lax.all_to_all(sent, "snp", split_axis=0, concat_axis=0, tiled=True)
-    scratch = [wide, pltpu.VMEM((4, 4, block // 4, 2 * samples), BF16), pltpu.VMEM((2 * samples, 2 * block), BF16)]
+    left = jax.ShapeDtypeStruct((4, 4, block // 4, samples), BF16)
+    right = jax.ShapeDtypeStruct((samples, 2 * block), BF16)
+    own_left0, own_left1, own_right0, own_right1, other_left1, other_right1 = run(
+        prepare_kernel, (marked, own1, other1, labels), [left, left, right, right, left, right], [wide])
     short = jax.ShapeDtypeStruct((block + 8, block), jnp.int32)
     tall = jax.ShapeDtypeStruct((block + 8 + pairs, block), jnp.int32)
-    *ahead, sums = run(
-        ahead_kernel, (marked, own1, other0, other1, labels),
-        [short] * 4 + [jax.ShapeDtypeStruct((8, 2 * block), F32)], scratch,
+    *ahead, sums, other_right0 = run(
+        ahead_kernel, (other0, own1, own_right0, own_right1, other_left1, labels),
+        [short] * 4 + [jax.ShapeDtypeStruct((8, 2 * block), F32), right], [wide, pltpu.VMEM(left.shape, BF16)],
     )
     for d in range(4):
         ahead[d] = moved(ahead[d], lambda b, k: (b - 1 - (k & 1), k ^ d))
     behind = run(
         functools.partial(behind_kernel, shift=shift),
-        (marked, own1, other0, other1, labels, own_ids, peer_ids, got, sums),
-        [tall] * 4, scratch,
+        (own1, own_left0, own_left1, own_right0, other_right0, other_right1, labels, own_ids, peer_ids, got, sums),
+        [tall] * 4, [],
     )
     behind = list(behind)
     for d in range(1, 4):

time: 58.7 us -> 57.9 us (0.986)
    pallas_call x4 -> x5, Pallas kernels: 5.51 us -> 5.17 us  [run(): pl.pallas_call(body, out_shape=[pltpu.VMEM(o.shape, o.dtype) if near else...]
where the time goes in v5:
time: 57.9 us; the launch traced here: 57.4 us
  waiting for transfers between devices  19.7 us (34%)
  starting transfers between devices  16.2 us (28%)
  blocking collectives  14.6 us (25%)
  Pallas kernels  6.22 us (11%)
  between operations  0.71 us (1%)
    ppermute x10, waiting for transfers between devices, moved(): return lax.ppermute(value, ('snp', 'samp'), links)  19.7 us
    ppermute x10, starting transfers between devices, moved(): return lax.ppermute(value, ('snp', 'samp'), links)  16.2 us
    all_to_all x1, blocking collectives, on_device(): got = lax.all_to_all(sent, 'snp', split_axis=0, concat_axis=0, tiled=True)  8.22 us
    psum x1, blocking collectives, on_device(): ids = lax.psum(placed, 'snp')  6.36 us
    pallas_call x5, Pallas kernels, run(): pl.pallas_call(body, out_shape=[pltpu.VMEM(o.shape, o.dtype) if near else...  5.17 us
  transfers between devices with their start and end apart: 10, of which 2 were waited for; matrix products, arithmetic and copies ran while one was open for 0% of the time, Pallas kernels for 4%

profile of v5, /device:TPU:0, one launch (start us, length us, event | category | flops | bytes accessed | tf_op | source)
XLA Modules:
  0.0 57.4 jit_solution(2731457777444301805)
XLA Ops:
  0.6 0.0 copy-start
  0.6 1.1 %shard_map.59 = (bf16[1032,128]{1,0:T(8,128)(2,1)S(1)}, s32[1,512]{1,0:T(1,128)S(1)}, s32[1,16]{1,0:T(1,128)S(1)}, s32[1,16]{1,0:T(1,128)S(1)}, s32[8,16]{1,0:T(8,128)S(1)}) custom-call(bf16[1024,128]{1,0:T(8,128)(2,1)} %bitcast.9, s32[1,512]{1,0:T(1,128)} %bitcast.12, s32[1,16]{1,0:T(1,128)} %bitcast.13, s32[1,16]{1,0:T(1,128)} %bitcast.14), custom_call_target="tpu_custom_call" | custom-call | tf_op jit(solution)/shard_map/pallas_call | solution.py:415
  1.7 3.1 %collective-permute-start = (bf16[1032,128]{1,0:T(8,128)(2,1)S(1)}, bf16[1032,128]{1,0:T(8,128)(2,1)S(1)}, u32[]{:S(2)}, u32[]{:S(2)}) collective-permute-start(bf16[1032,128]{1,0:T(8,128)(2,1)S(1)} %get-tuple-element.25.own0.geno), channel_id=1, source_target_pairs={{0,1},{1,0},{2,3},{3,2},{4,5},{5,4},{6,7},{7,6},{8,9},{9,8},{10,11... | collective-permute-start | bytes 792584 | tf_op jit(solution)/shard_map/ppermute | solution.py:401
  4.8 0.0 copy-done
  4.8 1.4 %collective-permute-start.1 = (bf16[1024,128]{1,0:T(8,128)(2,1)S(1)}, bf16[1024,128]{1,0:T(8,128)(2,1)S(1)}, u32[]{:S(2)}, u32[]{:S(2)}) collective-permute-start(bf16[1024,128]{1,0:T(8,128)(2,1)S(1)} %bitcast.10), channel_id=1, source_target_pairs={{0,9},{1,4},{2,11},{3,6},{4,13},{5,8},{6,15},{7,10},{8,17},{9,12},... | collective-permute-start | bytes 786440 | tf_op jit(solution)/shard_map/ppermute | solution.py:401
  6.2 0.0 collective-permute-start.2
  6.2 11.5 %collective-permute-done.1.other1 = bf16[1024,128]{1,0:T(8,128)(2,1)S(1)} collective-permute-done((bf16[1024,128]{1,0:T(8,128)(2,1)S(1)}, bf16[1024,128]{1,0:T(8,128)(2,1)S(1)}, u32[]{:S(2)}, u32[]{:S(2)}) %collective-permute-start.1) | collective-permute-done | bytes 262176 | tf_op jit(solution)/shard_map/ppermute | solution.py:401
  17.7 0.0 collective-permute-done.own1
  17.7 0.5 shard_map.60
  18.2 0.0 collective-permute-done.2.other0
  18.2 1.0 %shard_map.61 = (s32[136,128]{1,0:T(8,128)S(1)}, s32[136,128]{1,0:T(8,128)S(1)}, s32[136,128]{1,0:T(8,128)S(1)}, s32[136,128]{1,0:T(8,128)S(1)}, f32[8,256]{1,0:T(8,128)S(1)}, /*index=5*/bf16[512,256]{1,0:T(8,128)(2,1)S(1)}) custom-call(bf16[1024,128]{1,0:T(8,128)(2,1)S(1)} %collective-permute-done.2.other0, ...), custom_call_target="tpu_custom_call" | custom-call | tf_op jit(solution)/shard_map/pallas_call | solution.py:359
  19.2 1.2 %collective-permute-start.6 = (s32[136,128]{1,0:T(8,128)S(1)}, s32[136,128]{1,0:T(8,128)S(1)}, u32[]{:S(2)}, u32[]{:S(2)}) collective-permute-start(s32[136,128]{1,0:T(8,128)S(1)} %get-tuple-element.42), channel_id=1, source_target_pairs={{0,28},{1,25},{2,30},{3,27},{4,0},{5,29},{6,2},{7,31},{8,4},{9,1},... | collective-permute-start | bytes 208904 | tf_op jit(solution)/shard_map/ppermute | solution.py:401
  20.4 4.0 %collective-permute-start.7 = (s32[136,128]{1,0:T(8,128)S(1)}, s32[136,128]{1,0:T(8,128)S(1)}, u32[]{:S(2)}, u32[]{:S(2)}) collective-permute-start(s32[136,128]{1,0:T(8,128)S(1)} %get-tuple-element.43), channel_id=1, source_target_pairs={{0,29},{1,24},{2,31},{3,26},{4,1},{5,28},{6,3},{7,30},{8,5},{9,0},... | collective-permute-start | bytes 208904 | tf_op jit(solution)/shard_map/ppermute | solution.py:401
  24.3 6.4 %psum.7.ids = s32[8,16]{1,0:T(8,128)S(1)} all-reduce(s32[8,16]{1,0:T(8,128)S(1)} %get-tuple-element.36), channel_id=1, replica_groups=mesh['snp'=8,'samp'=4] {'snp'}, use_global_device_ids=true, to_apply=%region_0.0 | all-reduce | flops 128 | bytes 1024 | tf_op jit(solution)/shard_map/psum | solution.py:419
  30.7 0.5 shard_map.62
  31.2 8.2 %all_to_all.11 = bf16[8,8,512]{2,1,0:T(8,128)(2,1)S(1)} all-to-all(bf16[8,8,512]{2,1,0:T(8,128)(2,1)S(1)} %bitcast.8), channel_id=1, replica_groups=mesh['snp'=8,'samp'=4] {'snp'}, dimensions={0} | all-to-all | bytes 131072 | tf_op jit(solution)/shard_map/all_to_all | solution.py:425
  39.4 1.2 %shard_map.63 = (s32[152,128]{1,0:T(8,128)S(1)}, s32[152,128]{1,0:T(8,128)S(1)}, s32[152,128]{1,0:T(8,128)S(1)}, s32[152,128]{1,0:T(8,128)S(1)}) custom-call(bf16[1032,128]{1,0:T(8,128)(2,1)S(1)} %collective-permute-done.own1, bf16[4,4,32,512]{3,2,1,0:T(8,128)(2,1)S(1)} %get-tuple-element.27.own_left0, ...), custom_call_target="tpu_custom_call" | custom-call | tf_op jit(solution)/shard_map/pallas_call | solution.py:359
  40.7 0.3 collective-permute-start.3
  41.0 2.6 %collective-permute-start.4 = (s32[152,128]{1,0:T(8,128)S(1)}, s32[152,128]{1,0:T(8,128)S(1)}, u32[]{:S(2)}, u32[]{:S(2)}) collective-permute-start(s32[152,128]{1,0:T(8,128)S(1)} %get-tuple-element.40), channel_id=1, source_target_pairs={{0,2},{1,3},{2,0},{3,1},{4,6},{5,7},{6,4},{7,5},{8,10},{9,11},{10,... | collective-permute-start | bytes 233480 | tf_op jit(solution)/shard_map/ppermute | solution.py:401
  43.6 1.5 %collective-permute-start.5 = (s32[152,128]{1,0:T(8,128)S(1)}, s32[152,128]{1,0:T(8,128)S(1)}, u32[]{:S(2)}, u32[]{:S(2)}) collective-permute-start(s32[152,128]{1,0:T(8,128)S(1)} %get-tuple-element.41), channel_id=1, source_target_pairs={{0,3},{1,2},{2,1},{3,0},{4,7},{5,6},{6,5},{7,4},{8,11},{9,10},{10,... | collective-permute-start | bytes 233480 | tf_op jit(solution)/shard_map/ppermute | solution.py:401
  45.1 0.0 collective-permute-done.6.a0
  45.1 0.4 collective-permute-start.8
  45.5 0.0 collective-permute-done.7.a1
  45.5 1.7 %collective-permute-start.9 = (s32[136,128]{1,0:T(8,128)S(1)}, s32[136,128]{1,0:T(8,128)S(1)}, u32[]{:S(2)}, u32[]{:S(2)}) collective-permute-start(s32[136,128]{1,0:T(8,128)S(1)} %get-tuple-element.45), channel_id=1, source_target_pairs={{0,31},{1,26},{2,29},{3,24},{4,3},{5,30},{6,1},{7,28},{8,7},{9,2},... | collective-permute-start | bytes 208904 | tf_op jit(solution)/shard_map/ppermute | solution.py:401
  47.2 8.2 %collective-permute-done.8.a2 = s32[136,128]{1,0:T(8,128)S(1)} collective-permute-done((s32[136,128]{1,0:T(8,128)S(1)}, s32[136,128]{1,0:T(8,128)S(1)}, u32[]{:S(2)}, u32[]{:S(2)}) %collective-permute-start.8) | collective-permute-done | bytes 69664 | tf_op jit(solution)/shard_map/ppermute | solution.py:401
  55.4 0.0 collective-permute-done.9.a3
  55.4 0.0 collective-permute-done.3.b1
  55.4 0.0 collective-permute-done.4.b2
  55.4 0.0 collective-permute-done.5.b3
  55.4 2.0 %shard_map.64 = (f32[32,4,128]{2,1,0:T(4,128)}, f32[1,16]{1,0:T(1,128)}) custom-call(s32[152,128]{1,0:T(8,128)S(1)} %get-tuple-element.38.b0, s32[152,128]{1,0:T(8,128)S(1)} %collective-permute-done.3.b1, s32[152,128]{1,0:T(8,128)S(1)} %collective-permute-done.4.b2, s32[152,128]{1,0:T(8,128)S(1)} %collective-permute-done.5.b3, ...), custom_call_target="tpu_custom_call" | custom-call | tf_op jit(solution)/shard_map/pallas_call | solution.py:359
Async XLA Ops:
  0.6 4.2 %copy-start = (bf16[512,2,128]{2,1,0:T(2,128)(2,1)S(1)}, bf16[512,2,128]{2,1,0:T(2,128)(2,1)}, u32[]{:S(2)}) copy-start(bf16[512,2,128]{2,1,0:T(2,128)(2,1)} %param.4) | copy-start | bytes 786436
  1.7 16.0 %collective-permute-start = (bf16[1032,128]{1,0:T(8,128)(2,1)S(1)}, bf16[1032,128]{1,0:T(8,128)(2,1)S(1)}, u32[]{:S(2)}, u32[]{:S(2)}) collective-permute-start(bf16[1032,128]{1,0:T(8,128)(2,1)S(1)} %get-tuple-element.25.own0.geno), channel_id=1, source_target_pairs={{0,1},{1,0},{2,3},{3,2},{4,5},{5,4},{6,7},{7,6},{8,9},{9,8},{10,11... | collective-permute-start | bytes 792584 | tf_op jit(solution)/shard_map/ppermute | solution.py:401
  4.8 12.9 %collective-permute-start.1 = (bf16[1024,128]{1,0:T(8,128)(2,1)S(1)}, bf16[1024,128]{1,0:T(8,128)(2,1)S(1)}, u32[]{:S(2)}, u32[]{:S(2)}) collective-permute-start(bf16[1024,128]{1,0:T(8,128)(2,1)S(1)} %bitcast.10), channel_id=1, source_target_pairs={{0,9},{1,4},{2,11},{3,6},{4,13},{5,8},{6,15},{7,10},{8,17},{9,12},... | collective-permute-start | bytes 786440 | tf_op jit(solution)/shard_map/ppermute | solution.py:401
  6.2 12.0 %collective-permute-start.2 = (bf16[1024,128]{1,0:T(8,128)(2,1)S(1)}, bf16[1024,128]{1,0:T(8,128)(2,1)S(1)}, u32[]{:S(2)}, u32[]{:S(2)}) collective-permute-start(bf16[1024,128]{1,0:T(8,128)(2,1)S(1)} %bitcast.11), channel_id=1, source_target_pairs={{0,4},{1,9},{2,6},{3,11},{4,8},{5,13},{6,10},{7,15},{8,12},{9,17},... | collective-permute-start | bytes 786440 | tf_op jit(solution)/shard_map/ppermute | solution.py:401
  19.2 25.9 %collective-permute-start.6 = (s32[136,128]{1,0:T(8,128)S(1)}, s32[136,128]{1,0:T(8,128)S(1)}, u32[]{:S(2)}, u32[]{:S(2)}) collective-permute-start(s32[136,128]{1,0:T(8,128)S(1)} %get-tuple-element.42), channel_id=1, source_target_pairs={{0,28},{1,25},{2,30},{3,27},{4,0},{5,29},{6,2},{7,31},{8,4},{9,1},... | collective-permute-start | bytes 208904 | tf_op jit(solution)/shard_map/ppermute | solution.py:401
  20.4 25.1 %collective-permute-start.7 = (s32[136,128]{1,0:T(8,128)S(1)}, s32[136,128]{1,0:T(8,128)S(1)}, u32[]{:S(2)}, u32[]{:S(2)}) collective-permute-start(s32[136,128]{1,0:T(8,128)S(1)} %get-tuple-element.43), channel_id=1, source_target_pairs={{0,29},{1,24},{2,31},{3,26},{4,1},{5,28},{6,3},{7,30},{8,5},{9,0},... | collective-permute-start | bytes 208904 | tf_op jit(solution)/shard_map/ppermute | solution.py:401
  40.7 14.7 %collective-permute-start.3 = (s32[152,128]{1,0:T(8,128)S(1)}, s32[152,128]{1,0:T(8,128)S(1)}, u32[]{:S(2)}, u32[]{:S(2)}) collective-permute-start(s32[152,128]{1,0:T(8,128)S(1)} %get-tuple-element.39), channel_id=1, source_target_pairs={{0,1},{1,0},{2,3},{3,2},{4,5},{5,4},{6,7},{7,6},{8,9},{9,8},{10,11... | collective-permute-start | bytes 233480 | tf_op jit(solution)/shard_map/ppermute | solution.py:401
  41.0 14.4 %collective-permute-start.4 = (s32[152,128]{1,0:T(8,128)S(1)}, s32[152,128]{1,0:T(8,128)S(1)}, u32[]{:S(2)}, u32[]{:S(2)}) collective-permute-start(s32[152,128]{1,0:T(8,128)S(1)} %get-tuple-element.40), channel_id=1, source_target_pairs={{0,2},{1,3},{2,0},{3,1},{4,6},{5,7},{6,4},{7,5},{8,10},{9,11},{10,... | collective-permute-start | bytes 233480 | tf_op jit(solution)/shard_map/ppermute | solution.py:401
  43.6 11.8 %collective-permute-start.5 = (s32[152,128]{1,0:T(8,128)S(1)}, s32[152,128]{1,0:T(8,128)S(1)}, u32[]{:S(2)}, u32[]{:S(2)}) collective-permute-start(s32[152,128]{1,0:T(8,128)S(1)} %get-tuple-element.41), channel_id=1, source_target_pairs={{0,3},{1,2},{2,1},{3,0},{4,7},{5,6},{6,5},{7,4},{8,11},{9,10},{10,... | collective-permute-start | bytes 233480 | tf_op jit(solution)/shard_map/ppermute | solution.py:401
  45.1 10.3 %collective-permute-start.8 = (s32[136,128]{1,0:T(8,128)S(1)}, s32[136,128]{1,0:T(8,128)S(1)}, u32[]{:S(2)}, u32[]{:S(2)}) collective-permute-start(s32[136,128]{1,0:T(8,128)S(1)} %get-tuple-element.44), channel_id=1, source_target_pairs={{0,30},{1,27},{2,28},{3,25},{4,2},{5,31},{6,0},{7,29},{8,6},{9,3},... | collective-permute-start | bytes 208904 | tf_op jit(solution)/shard_map/ppermute | solution.py:401
  45.5 9.9 %collective-permute-start.9 = (s32[136,128]{1,0:T(8,128)S(1)}, s32[136,128]{1,0:T(8,128)S(1)}, u32[]{:S(2)}, u32[]{:S(2)}) collective-permute-start(s32[136,128]{1,0:T(8,128)S(1)} %get-tuple-element.45), channel_id=1, source_target_pairs={{0,31},{1,26},{2,29},{3,24},{4,3},{5,30},{6,1},{7,28},{8,7},{9,2},... | collective-permute-start | bytes 208904 | tf_op jit(solution)/shard_map/ppermute | solution.py:401
